TPU v7x, 256 devices: a whole 4x4x8 slice. The times are simulated.
256 devices in a mesh: ang: 32 (over y_lo, z, core), ax: 8 (over x, y_hi).
Axes of the slice: x: 4, y: 4 (y_hi: 2, y_lo: 2; y = y_hi * 2 + y_lo), z: 8, core: 2. Of those that a mesh axis runs over, the one named last changes fastest.
Arguments:
- concentration: float32 [3, 1024, 128, 512], P(None, 'ang', 'ax'), may hold values from 0.1 to 2
- courant: float32 [512], replicated, may hold values from 0.1 to 0.35
- axial_diffusion: float32 [3], replicated, may hold values from 0.05 to 0.12
- angular_rate: float32 [3, 512], replicated, may hold values from 0.05 to 0.18
- rate_constants: float32 [4], replicated, may hold values from 0.05 to 0.2
- species_map: int32 [4, 3], replicated, may hold values from 0 to 2, each once within a row
- wall_flags: int32 [3, 1024], P(None, 'ang'), may hold values 0 or 1
- radial_inverse: bfloat16 [3, 1024, 1024], replicated, may hold values from -1 to 1, as said below
Outputs:
- final_field: float32 [3, 1024, 128, 512], P(None, 'ang', 'ax')
Inputs may be any that keep to these rules, and one draw needn't show every extreme that they name: Every matrix is centrosymmetric: radial_inverse[s, i, j] equals radial_inverse[s, 1023 - i, 1023 - j].
All inputs are finite; a program needn't handle non-finite values. No bound on the sum of `wall_flags` on one device may be relied on, other than what follows from the above.
Results may differ from a plain program's by a relative error of at most 0.0029.
Values may be sent and summed in bfloat16 or wider, within the bound.
A program may use at most 64 MiB of HBM per device.

v0:
```python
import jax
import jax.numpy as jnp
from jax import lax
from jax.sharding import PartitionSpec as P

STEPS = 2


def extended(block, sides, width, periodic):
    for axis, dim in sides:
        count = lax.axis_size(axis)
        forward = [(i, i + 1) for i in range(count - 1)]
        if periodic:
            forward.append((count - 1, 0))
        backward = [(target, source) for source, target in forward]
        low = lax.ppermute(
            lax.slice_in_dim(block, block.shape[dim] - width, None, axis=dim), axis, forward
        )
        high = lax.ppermute(lax.slice_in_dim(block, 0, width, axis=dim), axis, backward)
        block = jnp.concatenate([low, block, high], axis=dim)
    return block


def swapped(value, axis, distance):
    mask = 2**distance
    pairs = [(source, source ^ mask) for source in range(lax.axis_size(axis))]
    return lax.ppermute(value, axis, pairs)


def product(matrix, values):
    return jnp.einsum("sij,sapj->sapi", matrix, values, preferred_element_type=jnp.float32)


def radial(matrices, mine, theirs):
    return product(matrices, jnp.concatenate((mine, theirs), 3))


def transport(field, courant, axial_diffusion, angular_rate, rate_constants, selectors, weights):
    angle_ext = extended(field, (("ang", 1),), 1, True)
    axial_ext = extended(field, (("ax", 2),), 1, False)
    angle_before = angle_ext[:, :-2]
    angle_after = angle_ext[:, 2:]
    axial_before = axial_ext[:, :, :-2]
    axial_after = axial_ext[:, :, 2:]
    reaction = jnp.zeros_like(field)
    for which_reaction in range(selectors.shape[0]):
        first_part = jnp.sum(selectors[which_reaction, 0][:, None, None, None] * field, axis=0)
        second_part = jnp.sum(selectors[which_reaction, 1][:, None, None, None] * field, axis=0)
        rate_term = rate_constants[which_reaction] * first_part * second_part
        reaction = reaction + weights[which_reaction][:, None, None, None] * rate_term[None]
    return (
        field
        - courant * (field - axial_before)
        + axial_diffusion[:, None, None, None] * (axial_after - 2.0 * field + axial_before)
        + angular_rate[:, None, None, :] * (angle_after - 2.0 * field + angle_before)
        + reaction
    )


def per_device(
    concentration,
    courant,
    axial_diffusion,
    angular_rate,
    rate_constants,
    species_map,
    wall_flags,
    radial_inverse,
):
    half_radial = concentration.shape[3]
    half_planes = concentration.shape[2] // 2
    species_count = concentration.shape[0]
    angle_count = lax.axis_size("ang")
    lower_half = lax.axis_index("ang") < angle_count // 2
    pair_bit = angle_count.bit_length() - 2
    species_ids = lax.broadcasted_iota(
        jnp.int32, (species_map.shape[0], species_map.shape[1], species_count), 2
    )
    selectors = (species_map[:, :, None] == species_ids).astype(jnp.float32)
    weights = selectors[:, 2] - selectors[:, 0] - selectors[:, 1]
    own_left = radial_inverse[:, :half_radial, :half_radial]
    own_right = radial_inverse[:, :half_radial, half_radial:][:, :, ::-1]
    back_left = radial_inverse[:, half_radial:, :half_radial][:, ::-1, :]
    back_right = radial_inverse[:, half_radial:, half_radial:][:, ::-1, ::-1]
    own_mats = jnp.concatenate((own_left, own_right), 2)
    back_mats = jnp.concatenate((back_left, back_right), 2)
    wall_mask = lax.broadcasted_iota(jnp.int32, concentration.shape, 3) == 0
    absorbing = wall_flags[:, :, None, None] == 1
    field = concentration
    for step_index in range(STEPS):
        explicit = transport(
            field, courant, axial_diffusion, angular_rate, rate_constants, selectors, weights
        )
        explicit_low = explicit.astype(jnp.bfloat16)
        first_planes = explicit_low[:, :, :half_planes]
        second_planes = explicit_low[:, :, half_planes:]
        kept = jnp.where(lower_half, first_planes, second_planes)
        sent = jnp.where(lower_half, second_planes, first_planes)
        theirs = swapped(sent, "ang", pair_bit)
        own_new = radial(own_mats, kept, theirs)
        back_new = radial(back_mats, kept, theirs)
        returned = swapped(back_new, "ang", pair_bit)
        updated = jnp.where(
            lower_half,
            jnp.concatenate((own_new, returned), 2),
            jnp.concatenate((returned, own_new), 2),
        )
        wall_value = jnp.where(absorbing, 0.0, updated[:, :, :, 1:2])
        field = jnp.where(wall_mask, wall_value, updated)
    return field


def solution(mesh):
    in_specs = (P(None, "ang", "ax", None), P(), P(), P(), P(), P(), P(None, "ang"), P())
    out_specs = P(None, "ang", "ax", None)
    return jax.shard_map(
        per_device, mesh=mesh, in_specs=in_specs, out_specs=out_specs, check_vma=False
    )
```

profile of v0, /device:TPU:230, one launch (start us, length us, event | category | flops | bytes accessed | tf_op | source)
XLA Modules:
  0.0 214.9 jit_solution(5692352405536601622)
XLA Ops:
  0.0 1.6 fusion.39
  1.6 0.4 collective-permute-start.2
  2.1 0.1 collective-permute-start.3
  2.1 2.3 %fusion.38 = (f32[3,32,1,512]{3,2,1,0:T(1,128)S(1)}, f32[3,32,1,512]{3,2,1,0:T(1,128)S(1)}) fusion(f32[3,32,16,512]{3,2,1,0:T(8,128)} %param.8), kind=kLoop, calls=%fused_computation.101 | loop fusion | bytes 786432 | tf_op jit(solution)/shard_map/slice | solution.py:17
  4.4 5.1 %collective-permute-start = (f32[3,32,1,512]{3,2,1,0:T(1,128)S(1)}, f32[3,32,1,512]{3,2,1,0:T(1,128)}, u32[]{:S(2)}, u32[]{:S(2)}) collective-permute-start(f32[3,32,1,512]{3,2,1,0:T(1,128)S(1)} %get-tuple-element.30), channel_id=1, source_target_pairs={{0,1},{1,2},{2,3},{3,4},{4,5},{5,6},{6,7},{8,9},{9,10},{10,11},{11... | collective-permute-start | bytes 589832 | tf_op jit(solution)/shard_map/ppermute | solution.py:16
  9.5 3.1 %collective-permute-start.1 = (f32[3,32,1,512]{3,2,1,0:T(1,128)S(1)}, f32[3,32,1,512]{3,2,1,0:T(1,128)}, u32[]{:S(2)}, u32[]{:S(2)}) collective-permute-start(f32[3,32,1,512]{3,2,1,0:T(1,128)S(1)} %get-tuple-element.31), channel_id=1, source_target_pairs={{1,0},{2,1},{3,2},{4,3},{5,4},{6,5},{7,6},{9,8},{10,9},{11,10},{12... | collective-permute-start | bytes 589832 | tf_op jit(solution)/shard_map/ppermute | solution.py:19
  12.7 0.8 fusion.30
  13.5 1.4 fusion.40
  15.0 4.4 %multiply_reduce_fusion.15 = (f32[32,16,512]{2,1,0:T(8,128)S(1)}, f32[32,16,512]{2,1,0:T(8,128)S(1)}, f32[32,16,512]{2,1,0:T(8,128)S(1)}, f32[32,16,512]{2,1,0:T...) fusion(f32[3,32,16,512]{3,2,1,0:T(8,128)} %param.8, ...), kind=kLoop, calls=%fused_computation.53 | loop fusion | flops 10485760 | bytes 11534432 | tf_op jit(solution)/shard_map/reduce_sum | solution.py:47
  19.4 3.1 %multiply_multiply_fusion.6 = (f32[32,16,512]{2,1,0:T(8,128)}, f32[32,16,512]{2,1,0:T(8,128)}) fusion(f32[32,16,512]{2,1,0:T(8,128)S(1)} %get-tuple-element.15, f32[32,16,512]{2,1,0:T(8,128)S(1)} %get-tuple-element.14, f32[]{:T(128)} %bitcast.5, f32[32,16,512]{2,1,0:T(8,128)S(1)} %get-tuple-element.18, f32[32,16,512]{2,1,0:T(8,128)S(1)} %get-tuple-element.13, ...), kind=kLoop, calls=%fused_computation.68 | loop fusion | flops 1048576 | bytes 6291464 | tf_op jit(solution)/shard_map/mul | solution.py:49
  22.5 3.4 %multiply_multiply_fusion.4 = (f32[32,16,512]{2,1,0:T(8,128)}, f32[32,16,512]{2,1,0:T(8,128)}) fusion(f32[32,16,512]{2,1,0:T(8,128)S(1)} %get-tuple-element.19, f32[32,16,512]{2,1,0:T(8,128)S(1)} %get-tuple-element.20, f32[]{:T(128)} %bitcast.13, f32[32,16,512]{2,1,0:T(8,128)S(1)} %get-tuple-element.17, f32[32,16,512]{2,1,0:T(8,128)S(1)} %get-tuple-element.16, ...), kind=kLoop, calls=%fused_computation.66 | loop fusion | flops 1048576 | bytes 6291464 | tf_op jit(solution)/shard_map/mul | solution.py:49
  25.9 0.6 slice_bitcast_fusion.11
  26.5 0.0 collective-permute-done.2
  26.5 0.0 collective-permute-done.3
  26.5 0.0 collective-permute-done
  26.5 0.0 collective-permute-done.1
  26.5 0.0 slice-start
  26.5 0.0 slice-start.1
  26.6 5.5 %fusion.17 = bf16[3,32,16,512]{3,2,1,0:T(8,128)(2,1)S(1)} fusion(f32[3,32,16,512]{3,2,1,0:T(8,128)S(1)} %copy-done, f32[3,1,16,512]{3,2,1,0:T(8,128)} %collective-permute-done.3, f32[3,1,16,512]{3,2,1,0:T(8,128)} %collective-permute-done.2, f32[3,32,1,512]{3,2,1,0:T(1,128)} %collective-permute-done.1, f32[3,32,1,512]{3,2,1,0:T(1,128)} %collective-permute-done, ...), kind=kLoop, calls=%fused_computation.22 | loop fusion | flops 19660800 | bytes 9510972 | tf_op jit(solution)/shard_map/convert_element_type | solution.py:94
  32.0 1.3 broadcast_select_fusion.5
  33.3 1.6 collective-permute-start.4
  34.9 2.2 %fusion.35 = (bf16[3,512,512]{2,1,0:T(8,128)(2,1)}, bf16[3,512,512]{2,1,0:T(8,128)(2,1)S(1)}, bf16[3,512,512]{2,1,0:T(8,128)(2,1)}, bf16[3,512,512]{2,1,0:T(8,128)(2,1)S(1)}) fusion(bf16[3,1024,1024]{2,1,0:T(8,128)(2,1)S(1)} %bitcast.45), kind=kLoop, calls=%fused_computation.98 | loop fusion | bytes 12582912 | tf_op jit(solution)/shard_map/slice | solution.py:81
  37.1 24.3 %rev.11 = bf16[3,512,512]{2,1,0:T(8,128)(2,1)} reverse(bf16[3,512,512]{2,1,0:T(8,128)(2,1)} %get-tuple-element.24), dimensions={1,2} | reverse | bytes 3145728 | tf_op jit(solution)/shard_map/rev | solution.py:84
  61.4 15.4 %rev.10 = bf16[3,512,512]{2,1,0:T(8,128)(2,1)} reverse(bf16[3,512,512]{2,1,0:T(8,128)(2,1)S(1)} %get-tuple-element.25), dimensions={1} | reverse | bytes 3145728 | tf_op jit(solution)/shard_map/rev | solution.py:83
  76.7 0.0 collective-permute-done.4
  76.7 4.6 %fusion.27 = f32[3,32,8,512]{3,2,1,0:T(8,128)} fusion(bf16[3,512,512]{2,1,0:T(8,128)(2,1)} %rev.11, bf16[3,512,512]{2,1,0:T(8,128)(2,1)} %rev.10, bf16[3,32,8,512]{3,2,1,0:T(8,128)(2,1)} %collective-permute-done.4, bf16[3,32,8,512]{3,2,1,0:T(8,128)(2,1)} %get-tuple-element.36), kind=kOutput, calls=%fused_computation.55 | convolution fusion | flops 814743552 | bytes 6291456 | tf_op jit(solution)/shard_map/sij,sapj->sapi/dot_general | solution.py:31
  81.3 0.4 collective-permute-start.5
  81.7 17.0 %rev.9 = bf16[3,512,512]{2,1,0:T(8,128)(2,1)} reverse(bf16[3,512,512]{2,1,0:T(8,128)(2,1)S(1)} %get-tuple-element.23), dimensions={2} | reverse | bytes 3145728 | tf_op jit(solution)/shard_map/rev | solution.py:82
  98.7 0.0 copy-done.28
  98.7 2.9 %fusion.29 = f32[3,32,8,512]{3,2,1,0:T(8,128)S(1)} fusion(bf16[3,512,512]{2,1,0:T(8,128)(2,1)} %rev.9, bf16[3,512,512]{2,1,0:T(8,128)(2,1)S(1)} %copy-done.1, bf16[3,32,8,512]{3,2,1,0:T(8,128)(2,1)} %collective-permute-done.4, bf16[3,32,8,512]{3,2,1,0:T(8,128)(2,1)} %get-tuple-element.36), kind=kOutput, calls=%fused_computation.57 | convolution fusion | flops 814743552 | bytes 6291456 | tf_op jit(solution)/shard_map/sij,sapj->sapi/dot_general | solution.py:31
  101.7 15.8 %collective-permute-done.5 = f32[3,32,8,512]{3,2,1,0:T(8,128)} collective-permute-done((f32[3,32,8,512]{3,2,1,0:T(8,128)}, f32[3,32,8,512]{3,2,1,0:T(8,128)}, u32[]{:S(2)}, u32[]{:S(2)}) %collective-permute-start.5) | collective-permute-done | bytes 1572896 | tf_op jit(solution)/shard_map/ppermute | solution.py:27
  117.5 2.5 %maximum_select_fusion = f32[3,32,16,512]{3,2,1,0:T(8,128)S(1)} fusion(f32[3,32,8,512]{3,2,1,0:T(8,128)} %collective-permute-done.5, f32[3,32,8,512]{3,2,1,0:T(8,128)S(1)} %fusion.29, pred[]{:T(512)S(6)} %lt.3), kind=kLoop, calls=%fused_computation.36 | loop fusion | flops 2359296 | bytes 6291457 | tf_op jit(solution)/shard_map/jit(_where)/select_n | solution.py:103
  120.1 1.3 slice_select_fusion.1
  121.3 1.7 copy.15
  123.1 0.0 copy-done.14
  123.1 0.0 copy-done.16
  123.2 7.0 %multiply_reduce_fusion.7 = (f32[32,16,512]{2,1,0:T(8,128)S(1)}, f32[32,16,512]{2,1,0:T(8,128)S(1)}, f32[32,16,512]{2,1,0:T(8,128)S(1)}, f32[32,16,512]{2,1,0:T(...) fusion(f32[3]{0:T(128)S(1)} %copy-done.22, ...), kind=kLoop, calls=%fused_computation.45 | loop fusion | flops 11272192 | bytes 14686816 | tf_op jit(solution)/shard_map/reduce_sum | solution.py:47
  130.2 0.4 fusion.36
  130.6 0.7 collective-permute-start.8
  131.3 0.7 collective-permute-start.9
  132.0 4.6 %collective-permute-start.6 = (f32[3,32,1,512]{3,2,1,0:T(1,128)S(1)}, f32[3,32,1,512]{3,2,1,0:T(1,128)S(1)}, u32[]{:S(2)}, u32[]{:S(2)}) collective-permute-start(f32[3,32,1,512]{3,2,1,0:T(1,128)S(1)} %get-tuple-element.26), channel_id=1, source_target_pairs={{0,1},{1,2},{2,3},{3,4},{4,5},{5,6},{6,7},{8,9},{9,10},{10,11},{11... | collective-permute-start | bytes 589832 | tf_op jit(solution)/shard_map/ppermute | solution.py:16
  136.5 3.7 %collective-permute-start.7 = (f32[3,32,1,512]{3,2,1,0:T(1,128)S(1)}, f32[3,32,1,512]{3,2,1,0:T(1,128)S(1)}, u32[]{:S(2)}, u32[]{:S(2)}) collective-permute-start(f32[3,32,1,512]{3,2,1,0:T(1,128)S(1)} %get-tuple-element.27), channel_id=1, source_target_pairs={{1,0},{2,1},{3,2},{4,3},{5,4},{6,5},{7,6},{9,8},{10,9},{11,10},{12... | collective-permute-start | bytes 589832 | tf_op jit(solution)/shard_map/ppermute | solution.py:19
  140.2 0.9 multiply_multiply_fusion.3
  141.1 0.8 multiply_multiply_fusion.1
  142.0 0.0 copy-start.27
  142.0 0.8 multiply_multiply_fusion
  142.9 0.8 multiply_multiply_fusion.2
  143.7 0.0 collective-permute-done.8
  143.7 0.0 collective-permute-done.9
  143.7 0.0 collective-permute-done.6
  143.7 3.9 %collective-permute-done.7 = f32[3,32,1,512]{3,2,1,0:T(1,128)S(1)} collective-permute-done((f32[3,32,1,512]{3,2,1,0:T(1,128)S(1)}, f32[3,32,1,512]{3,2,1,0:T(1,128)S(1)}, u32[]{:S(2)}, u32[]{:S(2)}) %collective-permute-start.7) | collective-permute-done | bytes 196640 | tf_op jit(solution)/shard_map/ppermute | solution.py:19
  147.7 3.8 %fusion.4 = bf16[3,32,16,512]{3,2,1,0:T(8,128)(2,1)S(1)} fusion(f32[3,32,16,512]{3,2,1,0:T(8,128)S(1)} %get-tuple-element.21, f32[3,1,16,512]{3,2,1,0:T(8,128)S(1)} %collective-permute-done.9, f32[3,1,16,512]{3,2,1,0:T(8,128)S(1)} %collective-permute-done.8, f32[3,32,1,512]{3,2,1,0:T(1,128)S(1)} %collective-permute-done.7, ...), kind=kLoop, calls=%fused_computation.5 | loop fusion | flops 19660800 | bytes 9510972 | tf_op jit(solution)/shard_map/convert_element_type | solution.py:94
  151.5 0.1 broadcast_select_fusion.3
  151.6 0.8 collective-permute-start.10
  152.5 19.5 %collective-permute-done.10 = bf16[3,32,8,512]{3,2,1,0:T(8,128)(2,1)S(1)} collective-permute-done((bf16[3,32,8,512]{3,2,1,0:T(8,128)(2,1)S(1)}, bf16[3,32,8,512]{3,2,1,0:T(8,128)(2,1)S(1)}, u32[]{:S(2)}, u32[]{:S(2)}) %collective-permute-start.10) | collective-permute-done | bytes 786464 | tf_op jit(solution)/shard_map/ppermute | solution.py:27
  172.0 1.0 fusion.26
  173.0 0.8 collective-permute-start.11
  173.8 0.0 copy-done.5
  173.9 1.0 fusion.28
  174.9 34.6 %collective-permute-done.11 = f32[3,32,8,512]{3,2,1,0:T(8,128)S(1)} collective-permute-done((f32[3,32,8,512]{3,2,1,0:T(8,128)S(1)}, f32[3,32,8,512]{3,2,1,0:T(8,128)S(1)}, u32[]{:S(2)}, u32[]{:S(2)}) %collective-permute-start.11) | collective-permute-done | bytes 1572896 | tf_op jit(solution)/shard_map/ppermute | solution.py:27
  209.5 0.4 maximum_select_fusion.1
  209.9 1.3 slice_select_fusion
  211.1 1.7 copy.16
  212.9 2.0 broadcast_select_fusion
  (61 shorter events, 0.2 us)
Async XLA Ops:
  1.6 24.8 %collective-permute-start.2 = (f32[3,1,16,512]{3,2,1,0:T(8,128)}, f32[3,1,16,512]{3,2,1,0:T(8,128)}, u32[]{:S(2)}, u32[]{:S(2)}) collective-permute-start(f32[3,1,16,512]{3,2,1,0:T(8,128)} %get-tuple-element.32), channel_id=1, source_target_pairs={{8,0},{16,8},{24,16},{32,24},{40,32},{48,40},{56,48},{64,56},{72,6... | collective-permute-start | bytes 294920 | tf_op jit(solution)/shard_map/ppermute | solution.py:19
  2.1 24.4 %collective-permute-start.3 = (f32[3,1,16,512]{3,2,1,0:T(8,128)}, f32[3,1,16,512]{3,2,1,0:T(8,128)}, u32[]{:S(2)}, u32[]{:S(2)}) collective-permute-start(f32[3,1,16,512]{3,2,1,0:T(8,128)} %get-tuple-element.33), channel_id=1, source_target_pairs={{0,8},{8,16},{16,24},{24,32},{32,40},{40,48},{48,56},{56,64},{64,7... | collective-permute-start | bytes 294920 | tf_op jit(solution)/shard_map/ppermute | solution.py:16
  4.4 22.1 %collective-permute-start = (f32[3,32,1,512]{3,2,1,0:T(1,128)S(1)}, f32[3,32,1,512]{3,2,1,0:T(1,128)}, u32[]{:S(2)}, u32[]{:S(2)}) collective-permute-start(f32[3,32,1,512]{3,2,1,0:T(1,128)S(1)} %get-tuple-element.30), channel_id=1, source_target_pairs={{0,1},{1,2},{2,3},{3,4},{4,5},{5,6},{6,7},{8,9},{9,10},{10,11},{11... | collective-permute-start | bytes 589832 | tf_op jit(solution)/shard_map/ppermute | solution.py:16
  9.5 17.0 %collective-permute-start.1 = (f32[3,32,1,512]{3,2,1,0:T(1,128)S(1)}, f32[3,32,1,512]{3,2,1,0:T(1,128)}, u32[]{:S(2)}, u32[]{:S(2)}) collective-permute-start(f32[3,32,1,512]{3,2,1,0:T(1,128)S(1)} %get-tuple-element.31), channel_id=1, source_target_pairs={{1,0},{2,1},{3,2},{4,3},{5,4},{6,5},{7,6},{9,8},{10,9},{11,10},{12... | collective-permute-start | bytes 589832 | tf_op jit(solution)/shard_map/ppermute | solution.py:19
  13.5 5.9 %copy-start.11 = (f32[3]{0:T(128)}, f32[3]{0:T(128)S(1)}, u32[]{:S(2)}) copy-start(f32[3]{0:T(128)S(1)} %get-tuple-element.38) | copy-start | bytes 40
  13.5 5.9 %copy-start.13 = (f32[3]{0:T(128)}, f32[3]{0:T(128)S(1)}, u32[]{:S(2)}) copy-start(f32[3]{0:T(128)S(1)} %get-tuple-element.39) | copy-start | bytes 40
  13.5 5.9 %copy-start.15 = (f32[3]{0:T(128)}, f32[3]{0:T(128)S(1)}, u32[]{:S(2)}) copy-start(f32[3]{0:T(128)S(1)} %get-tuple-element.40) | copy-start | bytes 40
  13.5 5.9 %copy-start.17 = (f32[3]{0:T(128)}, f32[3]{0:T(128)S(1)}, u32[]{:S(2)}) copy-start(f32[3]{0:T(128)S(1)} %get-tuple-element.41) | copy-start | bytes 40
  13.5 5.9 %copy-start.19 = (f32[3]{0:T(128)}, f32[3]{0:T(128)S(1)}, u32[]{:S(2)}) copy-start(f32[3]{0:T(128)S(1)} %get-tuple-element.42) | copy-start | bytes 40
  13.5 5.9 %copy-start.21 = (f32[3]{0:T(128)}, f32[3]{0:T(128)S(1)}, u32[]{:S(2)}) copy-start(f32[3]{0:T(128)S(1)} %get-tuple-element.43) | copy-start | bytes 40
  13.5 5.9 %copy-start.23 = (f32[3]{0:T(128)}, f32[3]{0:T(128)S(1)}, u32[]{:S(2)}) copy-start(f32[3]{0:T(128)S(1)} %get-tuple-element.44) | copy-start | bytes 40
  13.5 5.9 %copy-start.25 = (f32[3]{0:T(128)}, f32[3]{0:T(128)S(1)}, u32[]{:S(2)}) copy-start(f32[3]{0:T(128)S(1)} %get-tuple-element.45) | copy-start | bytes 40
  22.5 4.0 %copy-start = (f32[3,32,16,512]{3,2,1,0:T(8,128)S(1)}, f32[3,32,16,512]{3,2,1,0:T(8,128)}, u32[]{:S(2)}) copy-start(f32[3,32,16,512]{3,2,1,0:T(8,128)} %param.8) | copy-start | bytes 9437188
  22.5 4.0 %copy-start.6 = (f32[3,512]{1,0:T(4,128)S(1)}, f32[3,512]{1,0:T(4,128)}, u32[]{:S(2)}) copy-start(f32[3,512]{1,0:T(4,128)} %param.11) | copy-start | bytes 18436
  22.5 4.0 %copy-start.7 = (f32[512]{0:T(512)S(1)}, f32[512]{0:T(512)}, u32[]{:S(2)}) copy-start(f32[512]{0:T(512)} %param.9) | copy-start | bytes 6148
  26.5 8.4 %slice-start = ((s8[6291456]{0:T(1024)(128)(4,1)}), s8[4194304]{0:T(1024)(128)(4,1)S(1)}, s32[]{:S(2)}) async-start(s8[6291456]{0:T(1024)(128)(4,1)} %bitcast.44), calls=%async_computation | async-start | bytes 8388608
  26.5 8.4 %slice-start.1 = ((s8[6291456]{0:T(1024)(128)(4,1)}), s8[2097152]{0:T(1024)(128)(4,1)S(1)}, s32[]{:S(2)}) async-start(s8[6291456]{0:T(1024)(128)(4,1)} %bitcast.44), calls=%async_computation.1 | async-start | bytes 4194304
  33.3 43.4 %collective-permute-start.4 = (bf16[3,32,8,512]{3,2,1,0:T(8,128)(2,1)}, bf16[3,32,8,512]{3,2,1,0:T(8,128)(2,1)}, u32[]{:S(2)}, u32[]{:S(2)}) collective-permute-start(bf16[3,32,8,512]{3,2,1,0:T(8,128)(2,1)} %get-tuple-element.37), channel_id=1, source_target_pairs={{0,128},{8,136},{16,144},{24,152},{32,160},{40,168},{48,176},{56,1... | collective-permute-start | bytes 2359304 | tf_op jit(solution)/shard_map/ppermute | solution.py:27
  81.3 17.4 %copy-start.28 = (s32[3,32]{1,0:T(4,128)S(1)}, s32[3,32]{1,0:T(4,128)}, u32[]{:S(2)}) copy-start(s32[3,32]{1,0:T(4,128)} %param.14) | copy-start | bytes 1156
  81.3 17.4 %copy-start.1 = (bf16[3,512,512]{2,1,0:T(8,128)(2,1)S(1)}, bf16[3,512,512]{2,1,0:T(8,128)(2,1)}, u32[]{:S(2)}) copy-start(bf16[3,512,512]{2,1,0:T(8,128)(2,1)} %get-tuple-element.22) | copy-start | bytes 4718596
  81.3 36.2 %collective-permute-start.5 = (f32[3,32,8,512]{3,2,1,0:T(8,128)}, f32[3,32,8,512]{3,2,1,0:T(8,128)}, u32[]{:S(2)}, u32[]{:S(2)}) collective-permute-start(f32[3,32,8,512]{3,2,1,0:T(8,128)} %fusion.27), channel_id=1, source_target_pairs={{0,128},{8,136},{16,144},{24,152},{32,160},{40,168},{48,176},{56,1... | collective-permute-start | bytes 4718600 | tf_op jit(solution)/shard_map/ppermute | solution.py:27
  101.6 21.5 %copy-start.12 = (f32[3]{0:T(128)S(1)}, f32[3]{0:T(128)}, u32[]{:S(2)}) copy-start(f32[3]{0:T(128)} %copy-done.11) | copy-start | bytes 40
  101.6 21.5 %copy-start.14 = (f32[3]{0:T(128)S(1)}, f32[3]{0:T(128)}, u32[]{:S(2)}) copy-start(f32[3]{0:T(128)} %copy-done.13) | copy-start | bytes 40
  101.6 21.5 %copy-start.16 = (f32[3]{0:T(128)S(1)}, f32[3]{0:T(128)}, u32[]{:S(2)}) copy-start(f32[3]{0:T(128)} %copy-done.15) | copy-start | bytes 40
  101.6 21.5 %copy-start.18 = (f32[3]{0:T(128)S(1)}, f32[3]{0:T(128)}, u32[]{:S(2)}) copy-start(f32[3]{0:T(128)} %copy-done.17) | copy-start | bytes 40
  101.6 21.5 %copy-start.20 = (f32[3]{0:T(128)S(1)}, f32[3]{0:T(128)}, u32[]{:S(2)}) copy-start(f32[3]{0:T(128)} %copy-done.19) | copy-start | bytes 40
  101.7 21.5 %copy-start.22 = (f32[3]{0:T(128)S(1)}, f32[3]{0:T(128)}, u32[]{:S(2)}) copy-start(f32[3]{0:T(128)} %copy-done.21) | copy-start | bytes 40
  101.7 21.5 %copy-start.24 = (f32[3]{0:T(128)S(1)}, f32[3]{0:T(128)}, u32[]{:S(2)}) copy-start(f32[3]{0:T(128)} %copy-done.23) | copy-start | bytes 40
  101.7 21.5 %copy-start.26 = (f32[3]{0:T(128)S(1)}, f32[3]{0:T(128)}, u32[]{:S(2)}) copy-start(f32[3]{0:T(128)} %copy-done.25) | copy-start | bytes 40
  130.6 13.1 %collective-permute-start.8 = (f32[3,1,16,512]{3,2,1,0:T(8,128)S(1)}, f32[3,1,16,512]{3,2,1,0:T(8,128)S(1)}, u32[]{:S(2)}, u32[]{:S(2)}) collective-permute-start(f32[3,1,16,512]{3,2,1,0:T(8,128)S(1)} %get-tuple-element.28), channel_id=1, source_target_pairs={{8,0},{16,8},{24,16},{32,24},{40,32},{48,40},{56,48},{64,56},{72,6... | collective-permute-start | bytes 294920 | tf_op jit(solution)/shard_map/ppermute | solution.py:19
  131.3 12.4 %collective-permute-start.9 = (f32[3,1,16,512]{3,2,1,0:T(8,128)S(1)}, f32[3,1,16,512]{3,2,1,0:T(8,128)S(1)}, u32[]{:S(2)}, u32[]{:S(2)}) collective-permute-start(f32[3,1,16,512]{3,2,1,0:T(8,128)S(1)} %get-tuple-element.29), channel_id=1, source_target_pairs={{0,8},{8,16},{16,24},{24,32},{32,40},{40,48},{48,56},{56,64},{64,7... | collective-permute-start | bytes 294920 | tf_op jit(solution)/shard_map/ppermute | solution.py:16
  132.0 11.7 %collective-permute-start.6 = (f32[3,32,1,512]{3,2,1,0:T(1,128)S(1)}, f32[3,32,1,512]{3,2,1,0:T(1,128)S(1)}, u32[]{:S(2)}, u32[]{:S(2)}) collective-permute-start(f32[3,32,1,512]{3,2,1,0:T(1,128)S(1)} %get-tuple-element.26), channel_id=1, source_target_pairs={{0,1},{1,2},{2,3},{3,4},{4,5},{5,6},{6,7},{8,9},{9,10},{10,11},{11... | collective-permute-start | bytes 589832 | tf_op jit(solution)/shard_map/ppermute | solution.py:16
  136.5 11.1 %collective-permute-start.7 = (f32[3,32,1,512]{3,2,1,0:T(1,128)S(1)}, f32[3,32,1,512]{3,2,1,0:T(1,128)S(1)}, u32[]{:S(2)}, u32[]{:S(2)}) collective-permute-start(f32[3,32,1,512]{3,2,1,0:T(1,128)S(1)} %get-tuple-element.27), channel_id=1, source_target_pairs={{1,0},{2,1},{3,2},{4,3},{5,4},{6,5},{7,6},{9,8},{10,9},{11,10},{12... | collective-permute-start | bytes 589832 | tf_op jit(solution)/shard_map/ppermute | solution.py:19
  142.0 5.7 %copy-start.8 = (f32[3]{0:T(128)S(1)}, f32[3]{0:T(128)}, u32[]{:S(2)}) copy-start(f32[3]{0:T(128)} %get-tuple-element.47) | copy-start | bytes 40
  142.0 5.6 %copy-start.9 = (f32[3]{0:T(128)S(1)}, f32[3]{0:T(128)}, u32[]{:S(2)}) copy-start(f32[3]{0:T(128)} %get-tuple-element.48) | copy-start | bytes 40
  142.0 5.6 %copy-start.10 = (f32[3]{0:T(128)S(1)}, f32[3]{0:T(128)}, u32[]{:S(2)}) copy-start(f32[3]{0:T(128)} %get-tuple-element.49) | copy-start | bytes 40
  142.0 5.6 %copy-start.27 = (f32[3]{0:T(128)S(1)}, f32[3]{0:T(128)}, u32[]{:S(2)}) copy-start(f32[3]{0:T(128)} %param.10) | copy-start | bytes 40
  151.5 20.5 %copy-start.3 = (bf16[3,512,512]{2,1,0:T(8,128)(2,1)S(1)}, bf16[3,512,512]{2,1,0:T(8,128)(2,1)}, u32[]{:S(2)}) copy-start(bf16[3,512,512]{2,1,0:T(8,128)(2,1)} %rev.11) | copy-start | bytes 4718596
  151.5 20.5 %copy-start.4 = (bf16[3,512,512]{2,1,0:T(8,128)(2,1)S(1)}, bf16[3,512,512]{2,1,0:T(8,128)(2,1)}, u32[]{:S(2)}) copy-start(bf16[3,512,512]{2,1,0:T(8,128)(2,1)} %rev.10) | copy-start | bytes 4718596
  151.6 20.3 %collective-permute-start.10 = (bf16[3,32,8,512]{3,2,1,0:T(8,128)(2,1)S(1)}, bf16[3,32,8,512]{3,2,1,0:T(8,128)(2,1)S(1)}, u32[]{:S(2)}, u32[]{:S(2)}) collective-permute-start(bf16[3,32,8,512]{3,2,1,0:T(8,128)(2,1)S(1)} %get-tuple-element.35), channel_id=1, source_target_pairs={{0,128},{8,136},{16,144},{24,152},{32,160},{40,168},{48,176},{56,1... | collective-permute-start | bytes 2359304 | tf_op jit(solution)/shard_map/ppermute | solution.py:27
  172.0 1.9 copy-start.2
  172.0 1.9 copy-start.5
  173.0 36.5 %collective-permute-start.11 = (f32[3,32,8,512]{3,2,1,0:T(8,128)S(1)}, f32[3,32,8,512]{3,2,1,0:T(8,128)S(1)}, u32[]{:S(2)}, u32[]{:S(2)}) collective-permute-start(f32[3,32,8,512]{3,2,1,0:T(8,128)S(1)} %fusion.26), channel_id=1, source_target_pairs={{0,128},{8,136},{16,144},{24,152},{32,160},{40,168},{48,176},{56,1... | collective-permute-start | bytes 4718600 | tf_op jit(solution)/shard_map/ppermute | solution.py:27
where the time goes:
time: 218 us; the launch traced here: 215 us
  waiting for transfers between devices  73.9 us (34%)
  local copies, waits for them, and re-layouts  68.7 us (32%)
  other arithmetic  40.2 us (18%)
  starting transfers between devices  22 us (10%)
  matrix products  9.49 us (4%)
    ppermute x4, waiting for transfers between devices, swapped(): return lax.ppermute(value, axis, pairs)  69.9 us
    rev x1, local copies, waits for them, and re-layouts, per_device(): back_right = radial_inverse[:, half_radial:, half_radial:][:, ::-1, ::-1]  24.3 us
    rev x1, local copies, waits for them, and re-layouts, per_device(): own_right = radial_inverse[:, :half_radial, half_radial:][:, :, ::-1]  17 us
    rev x1, local copies, waits for them, and re-layouts, per_device(): back_left = radial_inverse[:, half_radial:, :half_radial][:, ::-1, :]  15.4 us
    reduce_sum x2, other arithmetic, transport(): jnp.sum(selectors[which_reaction, 0][:, None, None, None] * field, axis=0)  11.4 us
    ppermute x4, starting transfers between devices, extended(): lax.ppermute(lax.slice_in_dim(block, block.shape[dim] - width, None, axis...  10.4 us
    mul x6, other arithmetic, transport(): rate_term = rate_constants[which_reaction] * first_part * second_part  9.86 us
    dot_general x4, matrix products, product(): jnp.einsum('sij,sapj->sapi', matrix, values, preferred_element_type=jnp.f...  9.49 us
  transfers between devices with their start and end apart: 12, of which 4 were waited for; matrix products, arithmetic and copies ran while one was open for 38% of the time, Pallas kernels for 0%

commit v1 on v0

v1 whole, which is shorter than its diff:
```python
import functools

import jax
import jax.numpy as jnp
from jax import lax
from jax.experimental import pallas as pl
from jax.experimental.pallas import tpu as pltpu
from jax.sharding import PartitionSpec as P

MESH = pl.DeviceIdType.MESH
F32, BF16 = jnp.float32, jnp.bfloat16
LANES = 128
H = 2


def comm_kernel(
    conc, courant, ang_rate, ax_diff, rates, smap, flags, rinv,
    diam_out, w_out,
    o0, o1, t0, t1, ob, d1, d2, w, ma, ml, coef, hxf, pkf, pkb, hx, pa, ha, fl, fl_other, keep,
    load_sem, x_send, x_recv, hx_send, hx_recv, a_send, a_recv, fl_sem, m_sem, w_sem, d_sem,
):
    species, _, planes, radial = o0.shape
    angles = ob.shape[1]
    chunks = angles // (2 * H)
    rows_q = 2 * H
    per_blk = species * rows_q
    ang, ax = lax.axis_index("ang"), lax.axis_index("ax")
    n_ang, n_ax = lax.axis_size("ang"), lax.axis_size("ax")
    opp = lax.rem(ang + n_ang // 2, n_ang)
    up, down = lax.rem(ang + 1, n_ang), lax.rem(ang + n_ang - 1, n_ang)
    has_low, has_high = ax > 0, ax < n_ax - 1
    peer = {"ang": opp, "ax": ax}
    ang_peers = ({"ang": up, "ax": ax}, {"ang": down, "ax": ax})
    ax_peers = ({"ang": opp, "ax": ax + 1}, {"ang": opp, "ax": ax - 1})
    has_to, has_from = (has_high, has_low), (has_low, has_high)
    own, other = (o0, o1), (t0, t1)

    def low(j):
        return j * H

    def high(j):
        return angles - (j + 1) * H

    def angle(j, q):
        return j * H + q if q < H else angles - (j + 1) * H + q - H

    def load(j, end):
        start = (low, high)[end](j)
        return pltpu.make_async_copy(
            conc.at[:, pl.ds(start, H)], o0.at[:, pl.ds(start + 1, H)], load_sem.at[j, end]
        )

    def exchange(j, end):
        start = (low, high)[end](j)
        return pltpu.make_async_remote_copy(
            ob.at[:, pl.ds(start, H)], t0.at[:, pl.ds(start + 1, H)],
            x_send.at[j, end], x_recv.at[j, end], device_id=peer, device_id_type=MESH,
        )

    def ax_copy(step, j, side):
        return pltpu.make_async_remote_copy(
            pkb.at[step, j, side], hx.at[step, j, side],
            hx_send.at[step, j, side], hx_recv.at[step, j, side],
            device_id=ax_peers[side], device_id_type=MESH,
        )

    def ang_copies(step, side):
        t = other[step]
        source, target = ((angles, 0), (1, angles + 1))[side]
        return (
            pltpu.make_async_remote_copy(
                pa.at[step, side], ha.at[step, side],
                a_send.at[step, side, 0], a_recv.at[step, side, 0],
                device_id=ang_peers[side], device_id_type=MESH,
            ),
            pltpu.make_async_remote_copy(
                t.at[:, source], t.at[:, target],
                a_send.at[step, side, 1], a_recv.at[step, side, 1],
                device_id=ang_peers[side], device_id_type=MESH,
            ),
        )

    def flag_copy():
        return pltpu.make_async_remote_copy(
            fl, fl_other, fl_sem.at[0], fl_sem.at[1], device_id=peer, device_id_type=MESH
        )

    def diam_copy(j, end):
        start = (low, high)[end](j)
        return pltpu.make_async_copy(
            d2.at[:, pl.ds(start, H)], diam_out.at[:, pl.ds(start, H)], d_sem.at[j, end]
        )

    @pl.loop(0, chunks)
    def _(j):
        load(j, 0).start()
        load(j, 1).start()

    load_a = pltpu.make_async_copy(rinv.at[:, :radial, :radial], ma, m_sem.at[0])
    load_l = pltpu.make_async_copy(rinv.at[:, radial:, :radial], ml, m_sem.at[1])
    load_a.start()
    load_l.start()

    barrier = pltpu.get_barrier_semaphore()
    for device in (peer, *ang_peers):
        pl.semaphore_signal(barrier, inc=1, device_id=device, device_id_type=MESH)
    for side in range(2):

        @pl.when(has_to[side])
        def _():
            pl.semaphore_signal(barrier, inc=1, device_id=ax_peers[side], device_id_type=MESH)

    fl[...] = jnp.zeros_like(fl)
    fl[:species, :angles] = flags[...].astype(F32)
    for s in range(species):
        diffusion = ax_diff[s]
        coef[s, 0] = jnp.broadcast_to(
            1.0 - courant[...] - 2.0 * diffusion - 2.0 * ang_rate[s : s + 1], (planes, radial)
        )
        coef[s, 1] = jnp.broadcast_to(courant[...] + diffusion, (planes, radial))
        coef[s, 2] = jnp.broadcast_to(ang_rate[s : s + 1], (planes, radial))
    for side in range(2):

        @pl.when(jnp.logical_not(has_from[side]))
        def _():
            for step in range(2):

                @pl.loop(0, chunks)
                def _(j):
                    hx[step, j, side] = jnp.zeros(hx.shape[3:], BF16)

    gains = []
    for p in range(species):
        gain = jnp.float32(0.0)
        for k in range(rates.shape[0]):
            gain = gain + jnp.where(smap[k, 2] == p, rates[k], jnp.float32(0.0))
        gains.append(gain)

    def cast(j):
        for end in range(2):
            load(j, end).wait()
            start = (low, high)[end](j)
            for i in range(H):
                for s in range(species):
                    ob[s, start + i] = o0[s, start + i + 1].astype(BF16)

    cast(0)
    pl.semaphore_wait(barrier, 3 + jnp.where(has_low, 1, 0) + jnp.where(has_high, 1, 0))
    exchange(0, 0).start()
    exchange(0, 1).start()
    flag_copy().start()

    @pl.loop(1, chunks)
    def _(j):
        cast(j)
        exchange(j, 0).start()
        exchange(j, 1).start()

    load_a.wait()
    load_l.wait()
    flip = (
        lax.broadcasted_iota(jnp.int32, (radial, radial), 0)
        + lax.broadcasted_iota(jnp.int32, (radial, radial), 1)
        == radial - 1
    )
    flip = jnp.where(flip, 1.0, 0.0).astype(BF16)
    for s in range(species):
        w[s, :radial] = ma[s].T
        w[s, radial:] = jnp.dot(ml[s].T, flip, preferred_element_type=F32).astype(BF16)
    w_copy = pltpu.make_async_copy(w, w_out, w_sem.at[0])
    w_copy.start()

    flag_copy().wait_recv()
    diagonal = lax.broadcasted_iota(jnp.int32, (angles, LANES), 0) == lax.broadcasted_iota(
        jnp.int32, (angles, LANES), 1
    )
    for blk, ref in enumerate((fl, fl_other)):
        for s in range(species):
            row = jnp.broadcast_to(ref[s : s + 1], (angles, LANES))
            column = jnp.sum(jnp.where(diagonal, row, 0.0), axis=1, keepdims=True)
            rows = jnp.broadcast_to(1.0 - column, (angles, LANES))
            for a in range(angles):
                keep[blk, s, a] = jnp.broadcast_to(rows[a : a + 1], (planes, LANES))

    lane0 = lax.broadcasted_iota(jnp.int32, (planes, LANES), 1) == 0
    plane = lax.broadcasted_iota(jnp.int32, (planes, LANES), 0)
    first, last = plane == 0, plane == planes - 1

    def forward(step, j):
        for q in range(rows_q):
            a = angle(j, q) + 1
            for blk, ref in ((1, own[step]), (0, other[step])):
                for s in range(species):
                    value = ref[s, a].astype(F32)
                    row = slice(blk * per_blk + s * rows_q + q, blk * per_blk + s * rows_q + q + 1)
                    pkf[0, row, :] = value[planes - 1 : planes]
                    pkf[1, row, :] = value[0:1]

        for side in range(2):
            pkb[step, j, side] = pkf[side].astype(BF16)

            @pl.when(has_to[side])
            def _():
                ax_copy(step, j, side).start()

    def send_edges(step):
        for side in range(2):
            source = (angles, 1)[side]
            for s in range(species):
                pa[step, side, s] = own[step][s, source].astype(BF16)
            for copy in ang_copies(step, side):
                copy.start()

    def take_edges(step):
        for side in range(2):
            for copy in ang_copies(step, side):
                copy.wait_recv()
            target = (0, angles + 1)[side]
            for s in range(species):
                own[step][s, target] = ha[step, side, s].astype(F32)

    def explicit(step, j, store):
        for side in range(2):

            @pl.when(has_from[side])
            def _():
                ax_copy(step, j, side).wait_recv()

            hxf[side] = hx[step, j, side].astype(F32)

        for q in range(rows_q):
            a = angle(j, q) + 1
            for blk, ref in ((0, own[step]), (1, other[step])):
                for lane in range(0, radial, LANES):
                    sl = pl.ds(lane, LANES)
                    f = [ref[s, a, :, sl].astype(F32) for s in range(species)]
                    terms = [
                        gains[s] * (f[(s + 1) % species] * f[(s + 2) % species])
                        for s in range(species)
                    ]
                    total = terms[0] + terms[1] + terms[2]
                    for s in range(species):
                        row = slice(blk * per_blk + s * rows_q + q, blk * per_blk + s * rows_q + q + 1)
                        before = jnp.where(first, hxf[0, row, sl], pltpu.roll(f[s], 1, 0))
                        after = jnp.where(last, hxf[1, row, sl], pltpu.roll(f[s], planes - 1, 0))
                        angular = ref[s, a - 1, :, sl].astype(F32) + ref[s, a + 1, :, sl].astype(F32)
                        value = (
                            coef[s, 0, :, sl] * f[s]
                            + coef[s, 1, :, sl] * before
                            + ax_diff[s] * after
                            + coef[s, 2, :, sl] * angular
                            + (2.0 * terms[s] - total)
                        )
                        store(q, a, blk, s, lane, value.astype(BF16))

    def store_first(q, a, blk, s, lane, value):
        half = rows_q * planes
        sl = pl.ds(lane, LANES)
        offset = q * planes
        d1[s, pl.ds(blk * half + offset, planes), sl] = value
        if blk == 0:
            d1[s, pl.ds(2 * half + offset, planes), sl] = value

    def store_second(q, a, blk, s, lane, value):
        d2[s, a - 1, :, pl.ds(blk * radial + lane, LANES)] = value

    def implicit(j):
        half = rows_q * planes
        for s in range(species):
            y = jnp.dot(d1[s, : 2 * half], w[s, :radial], preferred_element_type=F32)
            y = y + jnp.dot(d1[s, half:], w[s, radial:], preferred_element_type=F32)
            for blk, ref in ((0, o1), (1, t1)):
                for q in range(rows_q):
                    a = angle(j, q)
                    part = y[blk * half + q * planes : blk * half + (q + 1) * planes]
                    head = part[:, :LANES]
                    wall = pltpu.roll(head, LANES - 1, 1) * keep[blk, s, a]
                    ref[s, a + 1, :, :LANES] = jnp.where(lane0, wall, head).astype(ref.dtype)
                    ref[s, a + 1, :, LANES:] = part[:, LANES:].astype(ref.dtype)

    @pl.loop(0, chunks + 2)
    def _(i):
        @pl.when(i < chunks)
        def _():
            exchange(i, 0).wait_recv()
            exchange(i, 1).wait_recv()
            forward(0, i)

            @pl.when(i == 0)
            def _():
                send_edges(0)

        @pl.when(jnp.logical_and(i >= 1, i <= chunks))
        def _():
            @pl.when(i == 1)
            def _():
                take_edges(0)

            explicit(0, i - 1, store_first)
            implicit(i - 1)
            forward(1, i - 1)

            @pl.when(i == 1)
            def _():
                send_edges(1)

        @pl.when(i >= 2)
        def _():
            @pl.when(i == 2)
            def _():
                take_edges(1)

            explicit(1, i - 2, store_second)
            diam_copy(i - 2, 0).start()
            diam_copy(i - 2, 1).start()

    w_copy.wait()
    flag_copy().wait_send()
    for step in range(2):
        for side in range(2):
            for copy in ang_copies(step, side):
                copy.wait_send()

    @pl.loop(0, chunks)
    def _(j):
        for end in range(2):
            exchange(j, end).wait_send()
            diam_copy(j, end).wait()
        for step in range(2):
            for side in range(2):

                @pl.when(has_to[side])
                def _():
                    ax_copy(step, j, side).wait_send()


def final_kernel(planes, flags, diam, w, out):
    radial = out.shape[2]
    s, block = pl.program_id(0), pl.program_id(1)
    y = jnp.dot(diam[0], w[0], preferred_element_type=F32)
    out[0] = y
    lane0 = lax.broadcasted_iota(jnp.int32, (planes, LANES), 1) == 0
    count = out.shape[1] // planes
    for i in range(count):
        head = y[i * planes : (i + 1) * planes, :LANES]
        wall = jnp.where(flags[s, block * count + i] == 1, 0.0, pltpu.roll(head, LANES - 1, 1))
        out[0, pl.ds(i * planes, planes), :LANES] = jnp.where(lane0, wall, head)


def per_device(
    concentration, courant, axial_diffusion, angular_rate, rate_constants, species_map, wall_flags, radial_inverse
):
    species, angles, planes, radial = concentration.shape
    chunks, rows_q = angles // (2 * H), 2 * H
    packed = 2 * species * rows_q
    vmem = pl.BlockSpec(memory_space=pltpu.VMEM)
    smem = pl.BlockSpec(memory_space=pltpu.SMEM)
    anywhere = pl.BlockSpec(memory_space=pl.ANY)
    dma = pltpu.SemaphoreType.DMA
    diam, w = pl.pallas_call(
        comm_kernel,
        out_shape=(
            jax.ShapeDtypeStruct((species, angles, planes, 2 * radial), BF16),
            jax.ShapeDtypeStruct((species, 2 * radial, radial), BF16),
        ),
        in_specs=[anywhere, vmem, vmem, smem, smem, smem, vmem, anywhere],
        out_specs=(anywhere, anywhere),
        scratch_shapes=[
            pltpu.VMEM((species, angles + 2, planes, radial), F32),
            pltpu.VMEM((species, angles + 2, planes, radial), F32),
            pltpu.VMEM((species, angles + 2, planes, radial), BF16),
            pltpu.VMEM((species, angles + 2, planes, radial), BF16),
            pltpu.VMEM((species, angles, planes, radial), BF16),
            pltpu.VMEM((species, 3 * rows_q * planes, radial), BF16),
            pltpu.VMEM((species, angles, planes, 2 * radial), BF16),
            pltpu.VMEM((species, 2 * radial, radial), BF16),
            pltpu.VMEM((species, radial, radial), BF16),
            pltpu.VMEM((species, radial, radial), BF16),
            pltpu.VMEM((species, 3, planes, radial), F32),
            pltpu.VMEM((2, packed, radial), F32),
            pltpu.VMEM((2, packed, radial), F32),
            pltpu.VMEM((2, chunks, 2, packed, radial), BF16),
            pltpu.VMEM((2, chunks, 2, packed, radial), BF16),
            pltpu.VMEM((2, 2, species, planes, radial), BF16),
            pltpu.VMEM((2, 2, species, planes, radial), BF16),
            pltpu.VMEM((8, LANES), F32),
            pltpu.VMEM((8, LANES), F32),
            pltpu.VMEM((2, species, angles, planes, LANES), F32),
            dma((chunks, 2)),
            dma((chunks, 2)),
            dma((chunks, 2)),
            dma((2, chunks, 2)),
            dma((2, chunks, 2)),
            dma((2, 2, 2)),
            dma((2, 2, 2)),
            dma((2,)),
            dma((2,)),
            dma((1,)),
            dma((chunks, 2)),
        ],
        compiler_params=pltpu.CompilerParams(
            collective_id=0, has_side_effects=True, vmem_limit_bytes=48 * 1024 * 1024
        ),
        name="steps",
    )(
        concentration, courant.reshape(1, radial), angular_rate, axial_diffusion, rate_constants,
        species_map, wall_flags, radial_inverse,
    )
    rows = angles * planes
    block = min(rows, 256)
    out = pl.pallas_call(
        functools.partial(final_kernel, planes),
        out_shape=jax.ShapeDtypeStruct((species, rows, radial), F32),
        grid=(species, rows // block),
        in_specs=[
            smem,
            pl.BlockSpec((1, block, 2 * radial), lambda s, b: (s, b, 0)),
            pl.BlockSpec((1, 2 * radial, radial), lambda s, b: (s, 0, 0)),
        ],
        out_specs=pl.BlockSpec((1, block, radial), lambda s, b: (s, b, 0)),
        compiler_params=pltpu.CompilerParams(vmem_limit_bytes=16 * 1024 * 1024),
        name="last",
    )(wall_flags, diam.reshape(species, rows, 2 * radial), w)
    return out.reshape(species, angles, planes, radial)


def solution(mesh):
    in_specs = (P(None, "ang", "ax", None), P(), P(), P(), P(), P(), P(None, "ang"), P())
    out_specs = P(None, "ang", "ax", None)
    return jax.shard_map(
        per_device, mesh=mesh, in_specs=in_specs, out_specs=out_specs, check_vma=False
    )
```

time: 218 us -> 66 us (0.30)
  the two profiles are of different devices: /device:TPU:230 before, /device:TPU:2 now
where the time goes in v1:
time: 66 us; the launch traced here: 65.7 us
  Pallas kernels  59.8 us (91%)
  local copies, waits for them, and re-layouts  5.93 us (9%)
    pallas_call x1, Pallas kernels, per_device(): pl.pallas_call(comm_kernel, out_shape=(jax.ShapeDtypeStruct((species, ang...  54.8 us
    unnamed x14, local copies, waits for them, and re-layouts  5.93 us
    pallas_call x1, Pallas kernels, per_device(): pl.pallas_call(functools.partial(final_kernel, planes), out_shape=jax.Sha...  5 us

profile of v1, /device:TPU:2, one launch (start us, length us, event | category | flops | bytes accessed | tf_op | source)
XLA Modules:
  0.0 65.7 jit_solution(14543221179983969161)
XLA Ops:
  0.0 0.0 copy-start.1
  0.0 0.7 %copy-done.1 = s32[3,32]{1,0:T(4,128)S(1)} copy-done((s32[3,32]{1,0:T(4,128)S(1)}, s32[3,32]{1,0:T(4,128)}, u32[]{:S(2)}) %copy-start.1) | copy-done | bytes 408
  0.7 0.0 copy-start.2
  0.7 0.7 %copy-done.2 = f32[3,512]{1,0:T(4,128)S(1)} copy-done((f32[3,512]{1,0:T(4,128)S(1)}, f32[3,512]{1,0:T(4,128)}, u32[]{:S(2)}) %copy-start.2) | copy-done | bytes 6168
  1.4 0.0 copy-start.3
  1.4 0.7 %copy-done.3 = f32[512]{0:T(512)S(1)} copy-done((f32[512]{0:T(512)S(1)}, f32[512]{0:T(512)}, u32[]{:S(2)}) %copy-start.3) | copy-done | bytes 2072
  2.1 0.0 copy-start.4
  2.1 0.7 %copy-done.4 = s32[4,3]{1,0:T(4,128)S(1)} copy-done((s32[4,3]{1,0:T(4,128)S(1)}, s32[4,3]{1,0:T(4,128)}, u32[]{:S(2)}) %copy-start.4) | copy-done | bytes 72
  2.7 0.0 copy-start.5
  2.7 0.7 copy-done.5
  3.4 0.0 copy-start.6
  3.4 0.7 copy-done.6
  4.1 54.8 %steps.1 = (bf16[3,32,16,1024]{3,2,1,0:T(8,128)(2,1)S(1)}, bf16[3,1024,512]{2,1,0:T(8,128)(2,1)}) custom-call(f32[3,32,16,512]{3,2,1,0:T(8,128)} %conc.1, f32[1,512]{1,0:T(1,128)S(1)} %bitcast.4, f32[3,512]{1,0:T(4,128)S(1)} %copy-done.2, f32[3]{0:T(128)S(1)} %copy-done.5, f32[4]{0:T(128)S(1)} %copy-done.6, s32[4,3]{1,0:T(4,128)S(1)} %copy-done.4, ...), custom_call_target="tpu_custom_call" | custom-call | tf_op jit(solution)/shard_map/steps/pallas_call | solution.py:360
  58.8 0.0 copy-start
  58.9 1.9 %copy-done = bf16[3,1024,512]{2,1,0:T(8,128)(2,1)S(1)} copy-done((bf16[3,1024,512]{2,1,0:T(8,128)(2,1)S(1)}, bf16[3,1024,512]{2,1,0:T(8,128)(2,1)}, u32[]{:S(2)}) %copy-start) | copy-done | bytes 3145752
  60.7 5.0 %last.1 = f32[3,512,512]{2,1,0:T(8,128)} custom-call(s32[3,32]{1,0:T(4,128)S(1)} %copy-done.1, bf16[3,512,1024]{2,1,0:T(8,128)(2,1)S(1)} %bitcast.3, bf16[3,1024,512]{2,1,0:T(8,128)(2,1)S(1)} %copy-done), custom_call_target="tpu_custom_call" | custom-call | tf_op jit(solution)/shard_map/last/pallas_call | solution.py:411
Async XLA Ops:
  0.0 0.7 %copy-start.1 = (s32[3,32]{1,0:T(4,128)S(1)}, s32[3,32]{1,0:T(4,128)}, u32[]{:S(2)}) copy-start(s32[3,32]{1,0:T(4,128)} %flags.3) | copy-start | bytes 1156
  0.7 0.7 %copy-start.2 = (f32[3,512]{1,0:T(4,128)S(1)}, f32[3,512]{1,0:T(4,128)}, u32[]{:S(2)}) copy-start(f32[3,512]{1,0:T(4,128)} %ang_rate.1) | copy-start | bytes 18436
  1.4 0.7 %copy-start.3 = (f32[512]{0:T(512)S(1)}, f32[512]{0:T(512)}, u32[]{:S(2)}) copy-start(f32[512]{0:T(512)} %param.9) | copy-start | bytes 6148
  2.1 0.7 %copy-start.4 = (s32[4,3]{1,0:T(4,128)S(1)}, s32[4,3]{1,0:T(4,128)}, u32[]{:S(2)}) copy-start(s32[4,3]{1,0:T(4,128)} %smap.1) | copy-start | bytes 148
  2.7 0.7 copy-start.5
  3.4 0.7 copy-start.6
  58.8 1.9 %copy-start = (bf16[3,1024,512]{2,1,0:T(8,128)(2,1)S(1)}, bf16[3,1024,512]{2,1,0:T(8,128)(2,1)}, u32[]{:S(2)}) copy-start(bf16[3,1024,512]{2,1,0:T(8,128)(2,1)} %get-tuple-element.8.w) | copy-start | bytes 9437188

commit v2 on v1

--- a/solution.py
+++ b/solution.py
@@ -1,5 +1,3 @@
-import functools
-
 import jax
 import jax.numpy as jnp
 from jax import lax
@@ -11,13 +9,15 @@
 F32, BF16 = jnp.float32, jnp.bfloat16
 LANES = 128
 H = 2
+VMEM_LIMIT = 40000000
 
 
 def comm_kernel(
-    conc, courant, ang_rate, ax_diff, rates, smap, flags, rinv,
-    diam_out, w_out,
-    o0, o1, t0, t1, ob, d1, d2, w, ma, ml, coef, hxf, pkf, pkb, hx, pa, ha, fl, fl_other, keep,
-    load_sem, x_send, x_recv, hx_send, hx_recv, a_send, a_recv, fl_sem, m_sem, w_sem, d_sem,
+    conc, courant_in, ang_rate_in, ax_diff_in, rates_in, smap_in, flags_in, rinv,
+    d2, w, keep_own,
+    courant, ang_rate, ax_diff, rates, smap, flags,
+    o0, o1, t0, t1, ob, d1, ma, ml, coef, hxf, pkf, pkb, hx, pa, ha, fl, fl_other, keep_other,
+    load_sem, x_send, x_recv, hx_send, hx_recv, a_send, a_recv, fl_sem, m_sem, p_sem,
 ):
     species, _, planes, radial = o0.shape
     angles = ob.shape[1]
@@ -85,11 +85,15 @@
             fl, fl_other, fl_sem.at[0], fl_sem.at[1], device_id=peer, device_id_type=MESH
         )
 
-    def diam_copy(j, end):
-        start = (low, high)[end](j)
-        return pltpu.make_async_copy(
-            d2.at[:, pl.ds(start, H)], diam_out.at[:, pl.ds(start, H)], d_sem.at[j, end]
-        )
+    small = [
+        pltpu.make_async_copy(source, target, p_sem.at[n])
+        for n, (source, target) in enumerate((
+            (courant_in, courant), (ang_rate_in, ang_rate), (ax_diff_in, ax_diff),
+            (rates_in, rates), (smap_in, smap), (flags_in, flags),
+        ))
+    ]
+    for copy in small:
+        copy.start()
 
     @pl.loop(0, chunks)
     def _(j):
@@ -110,6 +114,8 @@
         def _():
             pl.semaphore_signal(barrier, inc=1, device_id=ax_peers[side], device_id_type=MESH)
 
+    for copy in small:
+        copy.wait()
     fl[...] = jnp.zeros_like(fl)
     fl[:species, :angles] = flags[...].astype(F32)
     for s in range(species):
@@ -167,20 +173,19 @@
     for s in range(species):
         w[s, :radial] = ma[s].T
         w[s, radial:] = jnp.dot(ml[s].T, flip, preferred_element_type=F32).astype(BF16)
-    w_copy = pltpu.make_async_copy(w, w_out, w_sem.at[0])
-    w_copy.start()
 
     flag_copy().wait_recv()
     diagonal = lax.broadcasted_iota(jnp.int32, (angles, LANES), 0) == lax.broadcasted_iota(
         jnp.int32, (angles, LANES), 1
     )
+    keep = (keep_own, keep_other)
     for blk, ref in enumerate((fl, fl_other)):
         for s in range(species):
             row = jnp.broadcast_to(ref[s : s + 1], (angles, LANES))
             column = jnp.sum(jnp.where(diagonal, row, 0.0), axis=1, keepdims=True)
             rows = jnp.broadcast_to(1.0 - column, (angles, LANES))
             for a in range(angles):
-                keep[blk, s, a] = jnp.broadcast_to(rows[a : a + 1], (planes, LANES))
+                keep[blk][s, a] = jnp.broadcast_to(rows[a : a + 1], (planes, LANES))
 
     lane0 = lax.broadcasted_iota(jnp.int32, (planes, LANES), 1) == 0
     plane = lax.broadcasted_iota(jnp.int32, (planes, LANES), 0)
@@ -274,7 +279,7 @@
                     a = angle(j, q)
                     part = y[blk * half + q * planes : blk * half + (q + 1) * planes]
                     head = part[:, :LANES]
-                    wall = pltpu.roll(head, LANES - 1, 1) * keep[blk, s, a]
+                    wall = pltpu.roll(head, LANES - 1, 1) * keep[blk][s, a]
                     ref[s, a + 1, :, :LANES] = jnp.where(lane0, wall, head).astype(ref.dtype)
                     ref[s, a + 1, :, LANES:] = part[:, LANES:].astype(ref.dtype)
 
@@ -311,10 +316,7 @@
                 take_edges(1)
 
             explicit(1, i - 2, store_second)
-            diam_copy(i - 2, 0).start()
-            diam_copy(i - 2, 1).start()
-
-    w_copy.wait()
+
     flag_copy().wait_send()
     for step in range(2):
         for side in range(2):
@@ -325,7 +327,6 @@
     def _(j):
         for end in range(2):
             exchange(j, end).wait_send()
-            diam_copy(j, end).wait()
         for step in range(2):
             for side in range(2):
 
@@ -334,16 +335,19 @@
                     ax_copy(step, j, side).wait_send()
 
 
-def final_kernel(planes, flags, diam, w, out):
-    radial = out.shape[2]
+def final_kernel(diam, w, keep, out):
+    planes = keep.shape[2]
     s, block = pl.program_id(0), pl.program_id(1)
-    y = jnp.dot(diam[0], w[0], preferred_element_type=F32)
+    rows = out.shape[1]
+    count = rows // planes
+    y = jnp.dot(
+        diam[s, pl.ds(pl.multiple_of(block * rows, rows), rows)], w[s], preferred_element_type=F32
+    )
     out[0] = y
     lane0 = lax.broadcasted_iota(jnp.int32, (planes, LANES), 1) == 0
-    count = out.shape[1] // planes
     for i in range(count):
         head = y[i * planes : (i + 1) * planes, :LANES]
-        wall = jnp.where(flags[s, block * count + i] == 1, 0.0, pltpu.roll(head, LANES - 1, 1))
+        wall = pltpu.roll(head, LANES - 1, 1) * keep[s, block * count + i]
         out[0, pl.ds(i * planes, planes), :LANES] = jnp.where(lane0, wall, head)
 
 
@@ -354,26 +358,30 @@
     chunks, rows_q = angles // (2 * H), 2 * H
     packed = 2 * species * rows_q
     vmem = pl.BlockSpec(memory_space=pltpu.VMEM)
-    smem = pl.BlockSpec(memory_space=pltpu.SMEM)
-    anywhere = pl.BlockSpec(memory_space=pl.ANY)
+    hbm = pl.BlockSpec(memory_space=pltpu.HBM)
     dma = pltpu.SemaphoreType.DMA
-    diam, w = pl.pallas_call(
+    diam, w, keep = pl.pallas_call(
         comm_kernel,
         out_shape=(
-            jax.ShapeDtypeStruct((species, angles, planes, 2 * radial), BF16),
-            jax.ShapeDtypeStruct((species, 2 * radial, radial), BF16),
+            pltpu.VMEM((species, angles, planes, 2 * radial), BF16),
+            pltpu.VMEM((species, 2 * radial, radial), BF16),
+            pltpu.VMEM((species, angles, planes, LANES), F32),
         ),
-        in_specs=[anywhere, vmem, vmem, smem, smem, smem, vmem, anywhere],
-        out_specs=(anywhere, anywhere),
+        in_specs=[hbm] * 8,
+        out_specs=(vmem, vmem, vmem),
         scratch_shapes=[
+            pltpu.VMEM((1, radial), F32),
+            pltpu.VMEM((species, radial), F32),
+            pltpu.SMEM(axial_diffusion.shape, F32),
+            pltpu.SMEM(rate_constants.shape, F32),
+            pltpu.SMEM(species_map.shape, jnp.int32),
+            pltpu.VMEM((species, angles), jnp.int32),
             pltpu.VMEM((species, angles + 2, planes, radial), F32),
             pltpu.VMEM((species, angles + 2, planes, radial), F32),
             pltpu.VMEM((species, angles + 2, planes, radial), BF16),
             pltpu.VMEM((species, angles + 2, planes, radial), BF16),
             pltpu.VMEM((species, angles, planes, radial), BF16),
             pltpu.VMEM((species, 3 * rows_q * planes, radial), BF16),
-            pltpu.VMEM((species, angles, planes, 2 * radial), BF16),
-            pltpu.VMEM((species, 2 * radial, radial), BF16),
             pltpu.VMEM((species, radial, radial), BF16),
             pltpu.VMEM((species, radial, radial), BF16),
             pltpu.VMEM((species, 3, planes, radial), F32),
@@ -385,7 +393,7 @@
             pltpu.VMEM((2, 2, species, planes, radial), BF16),
             pltpu.VMEM((8, LANES), F32),
             pltpu.VMEM((8, LANES), F32),
-            pltpu.VMEM((2, species, angles, planes, LANES), F32),
+            pltpu.VMEM((species, angles, planes, LANES), F32),
             dma((chunks, 2)),
             dma((chunks, 2)),
             dma((chunks, 2)),
@@ -395,32 +403,32 @@
             dma((2, 2, 2)),
             dma((2,)),
             dma((2,)),
-            dma((1,)),
-            dma((chunks, 2)),
+            dma((6,)),
         ],
         compiler_params=pltpu.CompilerParams(
-            collective_id=0, has_side_effects=True, vmem_limit_bytes=48 * 1024 * 1024
+            collective_id=0, has_side_effects=True, vmem_limit_bytes=VMEM_LIMIT
         ),
         name="steps",
     )(
-        concentration, courant.reshape(1, radial), angular_rate, axial_diffusion, rate_constants,
-        species_map, wall_flags, radial_inverse,
+        *(
+            pltpu.with_memory_space_constraint(x, pltpu.HBM)
+            for x in (
+                concentration, courant.reshape(1, radial), angular_rate, axial_diffusion,
+                rate_constants, species_map, wall_flags, radial_inverse,
+            )
+        )
     )
     rows = angles * planes
     block = min(rows, 256)
     out = pl.pallas_call(
-        functools.partial(final_kernel, planes),
+        final_kernel,
         out_shape=jax.ShapeDtypeStruct((species, rows, radial), F32),
         grid=(species, rows // block),
-        in_specs=[
-            smem,
-            pl.BlockSpec((1, block, 2 * radial), lambda s, b: (s, b, 0)),
-            pl.BlockSpec((1, 2 * radial, radial), lambda s, b: (s, 0, 0)),
-        ],
+        in_specs=[vmem, vmem, vmem],
         out_specs=pl.BlockSpec((1, block, radial), lambda s, b: (s, b, 0)),
         compiler_params=pltpu.CompilerParams(vmem_limit_bytes=16 * 1024 * 1024),
         name="last",
-    )(wall_flags, diam.reshape(species, rows, 2 * radial), w)
+    )(diam.reshape(species, rows, 2 * radial), w, keep)
     return out.reshape(species, angles, planes, radial)
 
 

time: 66 us -> 58.8 us (0.89)
  local copies, waits for them, and re-layouts: 5.93 us -> 0 us
  Pallas kernels: 59.8 us -> 58.7 us
    unnamed x14 -> x0, local copies, waits for them, and re-layouts: 5.93 us -> none
    pallas_call x2, Pallas kernels: 59.8 us -> 58.7 us  [the longest x1 54.2 us: per_device(): pl.pallas_call(comm_kernel, out_shape=(pltpu.VMEM((species, angles, plane...]
where the time goes in v2:
time: 58.8 us; the launch traced here: 58.7 us
  Pallas kernels  58.7 us (100%)
    pallas_call x1, Pallas kernels, per_device(): pl.pallas_call(comm_kernel, out_shape=(pltpu.VMEM((species, angles, plane...  54.2 us
    pallas_call x1, Pallas kernels, per_device(): pl.pallas_call(final_kernel, out_shape=jax.ShapeDtypeStruct((species, row...  4.43 us

profile of v2, /device:TPU:2, one launch (start us, length us, event | category | flops | bytes accessed | tf_op | source)
XLA Modules:
  0.0 58.7 jit_solution(5866161231118449324)
XLA Ops:
  0.0 54.2 %steps.1 = (bf16[3,32,16,1024]{3,2,1,0:T(8,128)(2,1)S(1)}, bf16[3,1024,512]{2,1,0:T(8,128)(2,1)S(1)}, f32[3,32,16,128]{3,2,1,0:T(8,128)S(1)}) custom-call(f32[3,32,16,512]{3,2,1,0:T(8,128)} %conc.1, f32[1,512]{1,0:T(1,128)} %bitcast.4, f32[3,512]{1,0:T(4,128)} %ang_rate_in.1, f32[3]{0:T(128)} %ax_diff_in.1, f32[4]{0:T(128)} %rates_in.1, s32[4,3]{1,0:T(4,128)} %smap_in.1, ...), custom_call_target="tpu_custom_call" | custom-call | tf_op jit(solution)/shard_map/steps/pallas_call | solution.py:363
  54.2 4.4 %last.1 = f32[3,512,512]{2,1,0:T(8,128)} custom-call(bf16[3,512,1024]{2,1,0:T(8,128)(2,1)S(1)} %bitcast.3, bf16[3,1024,512]{2,1,0:T(8,128)(2,1)S(1)} %get-tuple-element.9.w, f32[3,32,16,128]{3,2,1,0:T(8,128)S(1)} %get-tuple-element.10.keep), custom_call_target="tpu_custom_call" | custom-call | tf_op jit(solution)/shard_map/last/pallas_call | solution.py:423

commit v3 on v2

v3 whole, which is shorter than its diff:
```python
import jax
import jax.numpy as jnp
from jax import lax
from jax.experimental import pallas as pl
from jax.experimental.pallas import tpu as pltpu
from jax.sharding import PartitionSpec as P

MESH = pl.DeviceIdType.MESH
F32, BF16 = jnp.float32, jnp.bfloat16
LANES = 128
H = 2
DIRECT = 3
VMEM_LIMIT = 40000000


def comm_kernel(
    conc, courant_in, ang_rate_in, ax_diff_in, rates_in, smap_in, flags_in, rinv,
    out,
    courant, ang_rate, ax_diff, rates, smap, flags,
    o0, o1, t0, t1, ob, d1, d2, w, ma, ml, coef, hxf, pkf, pko, pkt, pk1, hx0, hx1, pa, ha, fl, fl_other, keep,
    load_sem, x_send, x_recv, hxt_send, hxe_send, hx0_recv, hx1_send, hx1_recv, a_send, a_recv, fl_sem, m_sem, p_sem,
):
    species, _, planes, radial = o0.shape
    angles = ob.shape[1]
    chunks = angles // (2 * H)
    rows_q = 2 * H
    per_blk = species * rows_q
    forwarded = chunks - DIRECT
    ang, ax = lax.axis_index("ang"), lax.axis_index("ax")
    n_ang, n_ax = lax.axis_size("ang"), lax.axis_size("ax")
    opp = lax.rem(ang + n_ang // 2, n_ang)
    up, down = lax.rem(ang + 1, n_ang), lax.rem(ang + n_ang - 1, n_ang)
    has_low, has_high = ax > 0, ax < n_ax - 1
    peer = {"ang": opp, "ax": ax}
    ang_peers = ({"ang": up, "ax": ax}, {"ang": down, "ax": ax})
    ax_peers = ({"ang": opp, "ax": ax + 1}, {"ang": opp, "ax": ax - 1})
    ax_own = ({"ang": ang, "ax": ax + 1}, {"ang": ang, "ax": ax - 1})
    has_to, has_from = (has_high, has_low), (has_low, has_high)
    own, other = (o0, o1), (t0, t1)

    def angle(j, q):
        return j * H + q if q < H else angles - (j + 1) * H + q - H

    def remote(source, target, send, recv, device):
        return pltpu.make_async_remote_copy(
            source, target, send, recv, device_id=device, device_id_type=MESH
        )

    def load(j, end):
        start = (j * H, angles - (j + 1) * H)[end]
        return pltpu.make_async_copy(
            conc.at[:, pl.ds(start, H)], o0.at[:, pl.ds(start + 1, H)], load_sem.at[j, end]
        )

    def exchange(j, end, count):
        first = j * H + (0 if count > H else 1)
        start = (first, angles - first - count)[end]
        return remote(
            ob.at[:, pl.ds(start, count)], t0.at[:, pl.ds(start + 1, count)],
            x_send.at[j, end], x_recv.at[j, end], peer,
        )

    def each_exchange(i, act):
        for cond, count in ((i == 0, H + 1), ((i > 0) & (i < chunks - 1), H), (i == chunks - 1, H - 1)):

            @pl.when(cond)
            def _():
                act(exchange(i, 0, count))
                act(exchange(i, 1, count))

    def other_copy(j, side):
        return remote(
            pko.at[j, side], hx0.at[j, side, 1], hxt_send.at[j, side], hx0_recv.at[j, side, 1], ax_peers[side]
        )

    def own_copy(j, side, direct):
        return remote(
            (pko if direct else pkt).at[j, side], hx0.at[j, side, 0],
            hxe_send.at[j, side], hx0_recv.at[j, side, 0], (ax_own if direct else ax_peers)[side],
        )

    def second_copy(j, side):
        return remote(
            pk1.at[j, side], hx1.at[j, side], hx1_send.at[j, side], hx1_recv.at[j, side], ax_peers[side]
        )

    def ang_copies(step, side):
        t = other[step]
        source, target = ((angles, 0), (1, angles + 1))[side]
        return (
            remote(pa.at[step, side], ha.at[step, side], a_send.at[step, side, 0], a_recv.at[step, side, 0], ang_peers[side]),
            remote(t.at[:, source], t.at[:, target], a_send.at[step, side, 1], a_recv.at[step, side, 1], ang_peers[side]),
        )

    def flag_copy():
        return remote(fl, fl_other, fl_sem.at[0], fl_sem.at[1], peer)

    barrier = pltpu.get_barrier_semaphore()
    for device in (peer, *ang_peers):
        pl.semaphore_signal(barrier, inc=1, device_id=device, device_id_type=MESH)
    for side in range(2):

        @pl.when(has_to[side])
        def _():
            pl.semaphore_signal(barrier, inc=1, device_id=ax_peers[side], device_id_type=MESH)
            pl.semaphore_signal(barrier, inc=1, device_id=ax_own[side], device_id_type=MESH)

    for j in range(chunks):
        load(j, 0).start()
        load(j, 1).start()
    small = [
        pltpu.make_async_copy(source, target, p_sem.at[n])
        for n, (source, target) in enumerate((
            (courant_in, courant), (ang_rate_in, ang_rate), (ax_diff_in, ax_diff),
            (rates_in, rates), (smap_in, smap), (flags_in, flags),
        ))
    ]
    for copy in small:
        copy.start()
    load_a = pltpu.make_async_copy(rinv.at[:, :radial, :radial], ma, m_sem.at[0])
    load_l = pltpu.make_async_copy(rinv.at[:, radial:, :radial], ml, m_sem.at[1])
    load_a.start()
    load_l.start()

    def cast(j):
        for end in range(2):
            load(j, end).wait()
            start = (j * H, angles - (j + 1) * H)[end]
            for i in range(H):
                for s in range(species):
                    ob[s, start + i] = o0[s, start + i + 1].astype(BF16)

    cast(0)
    cast(1)
    for copy in small:
        copy.wait()
    fl[...] = jnp.zeros_like(fl)
    fl[:species, :angles] = flags[...].astype(F32)
    pl.semaphore_wait(barrier, 3 + jnp.where(has_low, 2, 0) + jnp.where(has_high, 2, 0))
    def pack(target, ref, j, per):
        for q in range(rows_q):
            a = angle(j, q) + 1
            for s in range(species):
                value = ref[s, a].astype(F32)
                row = slice(s * rows_q + q, s * rows_q + q + 1)
                pkf[per, 0, row, :] = value[planes - 1 : planes]
                pkf[per, 1, row, :] = value[0:1]
        for side in range(2):
            target(side)[...] = pkf[per, side].astype(BF16)

    def send(j):
        count = H + 1 if j == 0 else H if j < chunks - 1 else H - 1
        exchange(j, 0, count).start()
        exchange(j, 1, count).start()

    def send_planes(j, direct):
        pack(lambda side: pko.at[j, side], o0, j, 0)
        for side in range(2):

            @pl.when(has_to[side])
            def _():
                other_copy(j, side).start()
                if direct:
                    own_copy(j, side, True).start()

    flag_copy().start()
    send(0)
    for j in range(2, chunks):
        cast(j)
    for j in range(forwarded, chunks):
        send_planes(j, True)
    for j in range(1, chunks):
        send(j)

    @pl.loop(0, forwarded)
    def _(j):
        send_planes(j, False)

    for s in range(species):
        diffusion = ax_diff[s]
        coef[s, 0] = jnp.broadcast_to(
            1.0 - courant[...] - 2.0 * diffusion - 2.0 * ang_rate[s : s + 1], (planes, radial)
        )
        coef[s, 1] = jnp.broadcast_to(courant[...] + diffusion, (planes, radial))
        coef[s, 2] = jnp.broadcast_to(ang_rate[s : s + 1], (planes, radial))
    for side in range(2):

        @pl.when(jnp.logical_not(has_from[side]))
        def _():
            @pl.loop(0, chunks)
            def _(j):
                hx0[j, side] = jnp.zeros(hx0.shape[2:], BF16)
                hx1[j, side] = jnp.zeros(hx1.shape[2:], BF16)

    gains = []
    for p in range(species):
        gain = jnp.float32(0.0)
        for k in range(rates.shape[0]):
            gain = gain + jnp.where(smap[k, 2] == p, rates[k], jnp.float32(0.0))
        gains.append(gain)

    load_a.wait()
    load_l.wait()
    flip = (
        lax.broadcasted_iota(jnp.int32, (radial, radial), 0)
        + lax.broadcasted_iota(jnp.int32, (radial, radial), 1)
        == radial - 1
    )
    flip = jnp.where(flip, 1.0, 0.0).astype(BF16)
    for s in range(species):
        w[s, :radial] = ma[s].T
        w[s, radial:] = jnp.dot(ml[s].T, flip, preferred_element_type=F32).astype(BF16)

    flag_copy().wait_recv()
    diagonal = lax.broadcasted_iota(jnp.int32, (angles, LANES), 0) == lax.broadcasted_iota(
        jnp.int32, (angles, LANES), 1
    )
    for blk, ref in enumerate((fl, fl_other)):
        for s in range(species):
            row = jnp.broadcast_to(ref[s : s + 1], (angles, LANES))
            column = jnp.sum(jnp.where(diagonal, row, 0.0), axis=1, keepdims=True)
            rows = jnp.broadcast_to(1.0 - column, (angles, LANES))
            for a in range(angles):
                keep[blk, s, a] = jnp.broadcast_to(rows[a : a + 1], (planes, LANES))

    lane0 = lax.broadcasted_iota(jnp.int32, (planes, LANES), 1) == 0
    plane = lax.broadcasted_iota(jnp.int32, (planes, LANES), 0)
    first, last = plane == 0, plane == planes - 1
    half = rows_q * planes

    def send_edges(step):
        for side in range(2):
            source = (angles, 1)[side]
            for s in range(species):
                pa[step, side, s] = own[step][s, source].astype(BF16)
            for copy in ang_copies(step, side):
                copy.start()

    def take_edges(step):
        for side in range(2):
            for copy in ang_copies(step, side):
                copy.wait_recv()
            target = (0, angles + 1)[side]
            for s in range(species):
                own[step][s, target] = ha[step, side, s].astype(F32)

    def explicit(step, j):
        for side in range(2):

            @pl.when(has_from[side])
            def _():
                if step:
                    second_copy(j, side).wait_recv()
                else:
                    own_copy(j, side, True).wait_recv()
                    other_copy(j, side).wait_recv()

            for blk in range(2):
                hxf[side, blk] = (hx0, hx1)[step][j, side, blk].astype(F32)
        for q in range(rows_q):
            a = angle(j, q) + 1
            for blk, ref in ((0, own[step]), (1, other[step])):
                for lane in range(0, radial, LANES):
                    sl = pl.ds(lane, LANES)
                    f = [ref[s, a, :, sl].astype(F32) for s in range(species)]
                    terms = [
                        gains[s] * (f[(s + 1) % species] * f[(s + 2) % species])
                        for s in range(species)
                    ]
                    total = terms[0] + terms[1] + terms[2]
                    for s in range(species):
                        row = slice(s * rows_q + q, s * rows_q + q + 1)
                        before = jnp.where(first, hxf[0, blk, row, sl], pltpu.roll(f[s], 1, 0))
                        after = jnp.where(last, hxf[1, blk, row, sl], pltpu.roll(f[s], planes - 1, 0))
                        angular = ref[s, a - 1, :, sl].astype(F32) + ref[s, a + 1, :, sl].astype(F32)
                        value = (
                            coef[s, 0, :, sl] * f[s]
                            + coef[s, 1, :, sl] * before
                            + ax_diff[s] * after
                            + coef[s, 2, :, sl] * angular
                            + (2.0 * terms[s] - total)
                        ).astype(BF16)
                        rows = pl.ds(q * planes, planes)
                        if step:
                            d2[s, blk, lax.rem(j, 2), rows, sl] = value
                        else:
                            d1[s, blk, rows, sl] = value
                            if blk == 0:
                                d1[s, 2, rows, sl] = value

    def walled(ref, s, a, blk, part, offset):
        head = part[:, :LANES]
        wall = pltpu.roll(head, LANES - 1, 1) * keep[blk, s, a]
        ref[s, a + offset, :, :LANES] = jnp.where(lane0, wall, head).astype(ref.dtype)
        ref[s, a + offset, :, LANES:] = part[:, LANES:].astype(ref.dtype)

    def implicit_first(j):
        for s in range(species):
            mine = d1[s, :2].reshape(2 * half, radial)
            theirs = d1[s, 1:].reshape(2 * half, radial)
            y = jnp.dot(mine, w[s, :radial], preferred_element_type=F32)
            y = y + jnp.dot(theirs, w[s, radial:], preferred_element_type=F32)
            for blk, ref in ((0, o1), (1, t1)):
                for q in range(rows_q):
                    part = y[blk * half + q * planes : blk * half + (q + 1) * planes]
                    walled(ref, s, angle(j, q), blk, part, 1)

    def implicit_second(j):
        for s in range(species):
            y = jnp.dot(d2[s, 0].reshape(2 * half, radial), w[s, :radial], preferred_element_type=F32)
            y = y + jnp.dot(d2[s, 1].reshape(2 * half, radial), w[s, radial:], preferred_element_type=F32)
            for c in range(2):
                for q in range(rows_q):
                    part = y[c * half + q * planes : c * half + (q + 1) * planes]
                    walled(out, s, angle(j - 1 + c, q), 0, part, 0)

    def second_step(j):
        @pl.when(j == 0)
        def _():
            take_edges(1)

        explicit(1, j)

        @pl.when(lax.rem(j, 2) == 1)
        def _():
            implicit_second(j)

    inside = max(chunks - 4, 0)

    @pl.loop(0, chunks + 1)
    def _(i):
        @pl.when(i < forwarded)
        def _():
            each_exchange(i, lambda copy: copy.wait_recv())
            pack(lambda side: pkt.at[i, side], t0, i, 0)
            for side in range(2):

                @pl.when(has_to[side])
                def _():
                    own_copy(i, side, False).start()

            @pl.when(i == 0)
            def _():
                send_edges(0)

        if inside:

            @pl.when((i >= 3) & (i < 3 + inside))
            def _():
                second_step(i - 3)

        @pl.when(i >= 1)
        def _():
            @pl.when(i - 1 >= forwarded)
            def _():
                each_exchange(i - 1, lambda copy: copy.wait_recv())

            @pl.when(i == 1)
            def _():
                take_edges(0)

            explicit(0, i - 1)
            implicit_first(i - 1)
            pack(lambda side: pk1.at[i - 1, side, 1], o1, i - 1, 0)
            pack(lambda side: pk1.at[i - 1, side, 0], t1, i - 1, 1)
            for side in range(2):

                @pl.when(has_to[side])
                def _():
                    second_copy(i - 1, side).start()

            @pl.when(i == 1)
            def _():
                send_edges(1)

    @pl.loop(inside, chunks)
    def _(j):
        second_step(j)

    flag_copy().wait_send()
    for step in range(2):
        for side in range(2):
            for copy in ang_copies(step, side):
                copy.wait_send()

    @pl.loop(0, chunks)
    def _(j):
        each_exchange(j, lambda copy: copy.wait_send())
        for side in range(2):

            @pl.when(has_to[side])
            def _():
                other_copy(j, side).wait_send()
                own_copy(j, side, True).wait_send()
                second_copy(j, side).wait_send()


def per_device(
    concentration, courant, axial_diffusion, angular_rate, rate_constants, species_map, wall_flags, radial_inverse
):
    species, angles, planes, radial = concentration.shape
    chunks, rows_q = angles // (2 * H), 2 * H
    packed, half = species * rows_q, rows_q * planes
    hbm, vmem = pl.BlockSpec(memory_space=pltpu.HBM), pl.BlockSpec(memory_space=pltpu.VMEM)
    dma = pltpu.SemaphoreType.DMA
    return pl.pallas_call(
        comm_kernel,
        out_shape=pltpu.VMEM((species, angles, planes, radial), F32),
        in_specs=[hbm] * 8,
        out_specs=vmem,
        scratch_shapes=[
            pltpu.VMEM((1, radial), F32),
            pltpu.VMEM((species, radial), F32),
            pltpu.SMEM(axial_diffusion.shape, F32),
            pltpu.SMEM(rate_constants.shape, F32),
            pltpu.SMEM(species_map.shape, jnp.int32),
            pltpu.VMEM((species, angles), jnp.int32),
            pltpu.VMEM((species, angles + 2, planes, radial), F32),
            pltpu.VMEM((species, angles + 2, planes, radial), F32),
            pltpu.VMEM((species, angles + 2, planes, radial), BF16),
            pltpu.VMEM((species, angles + 2, planes, radial), BF16),
            pltpu.VMEM((species, angles, planes, radial), BF16),
            pltpu.VMEM((species, 3, half, radial), BF16),
            pltpu.VMEM((species, 2, 2, half, radial), BF16),
            pltpu.VMEM((species, 2 * radial, radial), BF16),
            pltpu.VMEM((species, radial, radial), BF16),
            pltpu.VMEM((species, radial, radial), BF16),
            pltpu.VMEM((species, 3, planes, radial), F32),
            pltpu.VMEM((2, 2, packed, radial), F32),
            pltpu.VMEM((2, 2, packed, radial), F32),
            pltpu.VMEM((chunks, 2, packed, radial), BF16),
            pltpu.VMEM((chunks, 2, packed, radial), BF16),
            pltpu.VMEM((chunks, 2, 2, packed, radial), BF16),
            pltpu.VMEM((chunks, 2, 2, packed, radial), BF16),
            pltpu.VMEM((chunks, 2, 2, packed, radial), BF16),
            pltpu.VMEM((2, 2, species, planes, radial), BF16),
            pltpu.VMEM((2, 2, species, planes, radial), BF16),
            pltpu.VMEM((8, LANES), F32),
            pltpu.VMEM((8, LANES), F32),
            pltpu.VMEM((2, species, angles, planes, LANES), F32),
            dma((chunks, 2)),
            dma((chunks, 2)),
            dma((chunks, 2)),
            dma((chunks, 2)),
            dma((chunks, 2)),
            dma((chunks, 2, 2)),
            dma((chunks, 2)),
            dma((chunks, 2)),
            dma((2, 2, 2)),
            dma((2, 2, 2)),
            dma((2,)),
            dma((2,)),
            dma((6,)),
        ],
        compiler_params=pltpu.CompilerParams(
            collective_id=0, has_side_effects=True, vmem_limit_bytes=VMEM_LIMIT
        ),
        name="steps",
    )(
        *(
            pltpu.with_memory_space_constraint(x, pltpu.HBM)
            for x in (
                concentration, courant.reshape(1, radial), angular_rate, axial_diffusion,
                rate_constants, species_map, wall_flags, radial_inverse,
            )
        )
    )


def solution(mesh):
    in_specs = (P(None, "ang", "ax", None), P(), P(), P(), P(), P(), P(None, "ang"), P())
    out_specs = P(None, "ang", "ax", None)
    return jax.shard_map(
        per_device, mesh=mesh, in_specs=in_specs, out_specs=out_specs, check_vma=False
    )
```

time: 58.8 us -> 56.6 us (0.963)
  Pallas kernels: 58.7 us -> 54.3 us
  local copies, waits for them, and re-layouts: 0 us -> 1.67 us
    pallas_call x2 -> x1, Pallas kernels: 58.7 us -> 54.3 us  [per_device(): pl.pallas_call(comm_kernel, out_shape=pltpu.VMEM((species, angles, planes...]
    unnamed x0 -> x1, local copies, waits for them, and re-layouts: none -> 1.67 us
where the time goes in v3:
time: 56.6 us; the launch traced here: 56 us
  Pallas kernels  54.3 us (96%)
  local copies, waits for them, and re-layouts  1.67 us (3%)
    pallas_call x1, Pallas kernels, per_device(): pl.pallas_call(comm_kernel, out_shape=pltpu.VMEM((species, angles, planes...  54.3 us
    unnamed x1, local copies, waits for them, and re-layouts  1.67 us

profile of v3, /device:TPU:2, one launch (start us, length us, event | category | flops | bytes accessed | tf_op | source)
XLA Modules:
  0.0 56.0 jit_solution(16970540402074558967)
XLA Ops:
  0.0 54.3 %steps.1 = f32[3,32,16,512]{3,2,1,0:T(8,128)S(1)} custom-call(f32[3,32,16,512]{3,2,1,0:T(8,128)} %conc.1, f32[1,512]{1,0:T(1,128)} %bitcast.1, f32[3,512]{1,0:T(4,128)} %ang_rate_in.1, f32[3]{0:T(128)} %ax_diff_in.1, f32[4]{0:T(128)} %rates_in.1, s32[4,3]{1,0:T(4,128)} %smap_in.1, s32[3,32]{1,0:T(4,128)} %flags_in.1, bf16[3,1024,1024]{2,1,0:T(8,128)(2,1)} %rinv.1), custom_call_target="tpu_custom_call" | custom-call | tf_op jit(solution)/shard_map/steps/pallas_call | solution.py:406
  54.3 1.7 %copy.10 = f32[3,32,16,512]{3,2,1,0:T(8,128)} copy(f32[3,32,16,512]{3,2,1,0:T(8,128)S(1)} %steps.1) | data formatting | bytes 6291456

commit v4 on v3

--- a/solution.py
+++ b/solution.py
@@ -29,7 +29,12 @@
     ang, ax = lax.axis_index("ang"), lax.axis_index("ax")
     n_ang, n_ax = lax.axis_size("ang"), lax.axis_size("ax")
     opp = lax.rem(ang + n_ang // 2, n_ang)
-    up, down = lax.rem(ang + 1, n_ang), lax.rem(ang + n_ang - 1, n_ang)
+    side_count = n_ang // 2
+    place = lax.rem(ang, side_count)
+    base = ang - place
+    up = base + lax.rem(place + 1, side_count)
+    down = base + lax.rem(place + side_count - 1, side_count)
+    wraps = (place == side_count - 1, place == 0)
     has_low, has_high = ax > 0, ax < n_ax - 1
     peer = {"ang": opp, "ax": ax}
     ang_peers = ({"ang": up, "ax": ax}, {"ang": down, "ax": ax})
@@ -84,12 +89,15 @@
             pk1.at[j, side], hx1.at[j, side], hx1_send.at[j, side], hx1_recv.at[j, side], ax_peers[side]
         )
 
-    def ang_copies(step, side):
+    def ang_copies(step, side, swapped=0):
         t = other[step]
         source, target = ((angles, 0), (1, angles + 1))[side]
-        return (
-            remote(pa.at[step, side], ha.at[step, side], a_send.at[step, side, 0], a_recv.at[step, side, 0], ang_peers[side]),
-            remote(t.at[:, source], t.at[:, target], a_send.at[step, side, 1], a_recv.at[step, side, 1], ang_peers[side]),
+        targets = (ha.at[step, side], t.at[:, target])
+        return tuple(
+            remote(
+                start, targets[n ^ swapped], a_send.at[step, side, n], a_recv.at[step, side, n ^ swapped], ang_peers[side]
+            )
+            for n, start in enumerate((pa.at[step, side], t.at[:, source]))
         )
 
     def flag_copy():
@@ -233,8 +241,12 @@
             source = (angles, 1)[side]
             for s in range(species):
                 pa[step, side, s] = own[step][s, source].astype(BF16)
-            for copy in ang_copies(step, side):
-                copy.start()
+            for swapped in range(2):
+
+                @pl.when(wraps[side] if swapped else jnp.logical_not(wraps[side]))
+                def _():
+                    for copy in ang_copies(step, side, swapped):
+                        copy.start()
 
     def take_edges(step):
         for side in range(2):

time: 56.6 us -> 53.9 us (0.952)
  Pallas kernels: 54.3 us -> 52.1 us
    pallas_call x1, Pallas kernels: 54.3 us -> 52.1 us  [per_device(): pl.pallas_call(comm_kernel, out_shape=pltpu.VMEM((species, angles, planes...]
where the time goes in v4:
time: 53.9 us; the launch traced here: 53.8 us
  Pallas kernels  52.1 us (97%)
  local copies, waits for them, and re-layouts  1.67 us (3%)
    pallas_call x1, Pallas kernels, per_device(): pl.pallas_call(comm_kernel, out_shape=pltpu.VMEM((species, angles, planes...  52.1 us
    unnamed x1, local copies, waits for them, and re-layouts  1.67 us

profile of v4, /device:TPU:2, one launch (start us, length us, event | category | flops | bytes accessed | tf_op | source)
XLA Modules:
  0.0 53.8 jit_solution(4050970967759937454)
XLA Ops:
  0.0 52.1 %steps.1 = f32[3,32,16,512]{3,2,1,0:T(8,128)S(1)} custom-call(f32[3,32,16,512]{3,2,1,0:T(8,128)} %conc.1, f32[1,512]{1,0:T(1,128)} %bitcast.1, f32[3,512]{1,0:T(4,128)} %ang_rate_in.1, f32[3]{0:T(128)} %ax_diff_in.1, f32[4]{0:T(128)} %rates_in.1, s32[4,3]{1,0:T(4,128)} %smap_in.1, s32[3,32]{1,0:T(4,128)} %flags_in.1, bf16[3,1024,1024]{2,1,0:T(8,128)(2,1)} %rinv.1), custom_call_target="tpu_custom_call" | custom-call | tf_op jit(solution)/shard_map/steps/pallas_call | solution.py:418
  52.2 1.7 %copy.10 = f32[3,32,16,512]{3,2,1,0:T(8,128)} copy(f32[3,32,16,512]{3,2,1,0:T(8,128)S(1)} %steps.1) | data formatting | bytes 6291456

commit v5 on v4

--- a/solution.py
+++ b/solution.py
@@ -9,7 +9,7 @@
 F32, BF16 = jnp.float32, jnp.bfloat16
 LANES = 128
 H = 2
-DIRECT = 3
+DIRECT = 2
 VMEM_LIMIT = 40000000
 
 

time: 53.9 us -> 53.3 us (0.989)
    pallas_call x1, Pallas kernels: 52.1 us -> 51.6 us  [per_device(): pl.pallas_call(comm_kernel, out_shape=pltpu.VMEM((species, angles, planes...]
where the time goes in v5:
time: 53.3 us
  Pallas kernels  51.6 us (97%)
  local copies, waits for them, and re-layouts  1.67 us (3%)
    pallas_call x1, Pallas kernels, per_device(): pl.pallas_call(comm_kernel, out_shape=pltpu.VMEM((species, angles, planes...  51.6 us
    unnamed x1, local copies, waits for them, and re-layouts  1.67 us

profile of v5, /device:TPU:2, one launch (start us, length us, event | category | flops | bytes accessed | tf_op | source)
XLA Modules:
  0.0 53.3 jit_solution(17807289443374937435)
XLA Ops:
  0.0 51.6 %steps.1 = f32[3,32,16,512]{3,2,1,0:T(8,128)S(1)} custom-call(f32[3,32,16,512]{3,2,1,0:T(8,128)} %conc.1, f32[1,512]{1,0:T(1,128)} %bitcast.1, f32[3,512]{1,0:T(4,128)} %ang_rate_in.1, f32[3]{0:T(128)} %ax_diff_in.1, f32[4]{0:T(128)} %rates_in.1, s32[4,3]{1,0:T(4,128)} %smap_in.1, s32[3,32]{1,0:T(4,128)} %flags_in.1, bf16[3,1024,1024]{2,1,0:T(8,128)(2,1)} %rinv.1), custom_call_target="tpu_custom_call" | custom-call | tf_op jit(solution)/shard_map/steps/pallas_call | solution.py:418
  51.6 1.7 %copy.10 = f32[3,32,16,512]{3,2,1,0:T(8,128)} copy(f32[3,32,16,512]{3,2,1,0:T(8,128)S(1)} %steps.1) | data formatting | bytes 6291456
